TPU v7x, 32 devices: a whole 2x2x4 slice. The times are simulated.
32 devices in a mesh: dp: 32 (over z, y, x, core).
Axes of the slice: x: 2, y: 2, z: 4, core: 2. Of those that a mesh axis runs over, the one named last changes fastest.
Arguments:
- tokens: bfloat16 [8192, 1152], P('dp'), may hold values from -6 to 6
- qkv_weights: bfloat16 [3981312], P('dp'), may hold values from -0.1875 to 0.1875
- out_weights: bfloat16 [1327104], P('dp'), may hold values from -3 to 3
- fc1_weights: bfloat16 [4958208], P('dp'), may hold values from -0.1875 to 0.1875
- fc2_weights: bfloat16 [4958208], P('dp'), may hold values from -0.09375 to 0.09375
- ln_gain: float32 [2, 1152], replicated, may hold values from 0.25 to 1.75
- bias_model: float32 [6, 1152], replicated, may hold values from -3 to 3
- first_feedforward_bias: float32 [4304], replicated, may hold values from -3 to 3
- qkv_down: bfloat16 [3, 1152, 128], replicated, may hold values from -0.1875 to 0.1875
- qkv_up: bfloat16 [3, 128, 1152], replicated, may hold values from -0.75 to 0.75
- out_down: bfloat16 [1152, 128], replicated, may hold values from -3 to 3
- out_up: bfloat16 [128, 1152], replicated, may hold values from -0.75 to 0.75
- first_feedforward_down: bfloat16 [1152, 128], replicated, may hold values from -0.1875 to 0.1875
- fc1_up: bfloat16 [128, 4304], replicated, may hold values from -0.75 to 0.75
- fc2_down: bfloat16 [4304, 128], replicated, may hold values from -0.09375 to 0.09375
- fc2_up: bfloat16 [128, 1152], replicated, may hold values from -0.75 to 0.75
- adapter_of_image: int32 [12], replicated, may hold values from 0 to 7
- cotangent: bfloat16 [8192, 1152], P('dp'), may hold values from -6 to 6
Outputs:
- output: bfloat16 [8192, 1152], P('dp')
- grad_tokens: bfloat16 [8192, 1152], P('dp')
- grad_qkv_down: float32 [442368], P('dp')
- grad_qkv_up: float32 [442368], P('dp')
- grad_out_down: float32 [147456], P('dp')
- grad_out_up: float32 [147456], P('dp')
- grad_fc1_down: float32 [147456], P('dp')
- grad_fc1_up: float32 [550912], P('dp')
- grad_fc2_down: float32 [550912], P('dp')
- grad_fc2_up: float32 [147456], P('dp')
All inputs are finite; a program needn't handle non-finite values.
Results may differ from a plain program's by a relative error of at most 0.015.
Values may be sent and summed in bfloat16 or wider, within the bound.
A program may use at most 256 MiB of HBM per device.

v0:
```python
from functools import partial

import jax
import jax.numpy as jnp
from jax import lax
from jax.sharding import PartitionSpec as P

D = 1152
HEADS = 16
HEAD_DIM = 72
FF = 4304
IMG = 729
RANK = 16
ADAPTERS = 8
REACH = 3
IMAGE_SLOTS = 2


epsilon = 1e-06


def shifted(value, axis, steps):
    count = lax.axis_size(axis)
    first, last = (max(0, -steps), min(count, count - steps))
    return lax.ppermute(value, axis, [(source, source + steps) for source in range(first, last)])


def norm_rows(inputs, gain_row, shift_row):
    center = inputs - jnp.mean(inputs, axis=-1, keepdims=True)
    spread_inv = lax.rsqrt(jnp.mean(center * center, axis=-1, keepdims=True) + epsilon)
    return center * spread_inv * gain_row + shift_row


def gelu_tanh(inputs):
    return (
        0.5
        * inputs
        * (1.0 + jnp.tanh(0.7978845608028654 * (inputs + 0.044715 * inputs * inputs * inputs)))
    )


def product(left, right):
    return jnp.dot(left, right, preferred_element_type=jnp.float32)


def inner_product(left, right):
    return lax.dot_general(
        left, right, (((0,), (0,)), ((), ())), preferred_element_type=jnp.float32
    )


def product_with_transpose(left, right):
    return lax.dot_general(
        left, right, (((1,), (1,)), ((), ())), preferred_element_type=jnp.float32
    )


def unpack(flat):
    return (
        flat[0].reshape(3, D, D),
        flat[1].reshape(D, D),
        flat[2].reshape(D, FF),
        flat[3].reshape(FF, D),
    )


def local(
    tokens,
    qkv_weights,
    out_weights,
    fc1_weights,
    fc2_weights,
    ln_gain,
    bias_model,
    first_feedforward_bias,
    qkv_down,
    qkv_up,
    out_down,
    out_up,
    first_feedforward_down,
    fc1_up,
    fc2_down,
    fc2_up,
    adapter_of_image,
    cotangent,
):
    local_rows = tokens.shape[0]
    devices = lax.axis_size("dp")
    all_tokens = local_rows * devices
    images = adapter_of_image.shape[0]
    row_start = lax.axis_index("dp") * local_rows
    positions = row_start + jnp.arange(local_rows, dtype=jnp.int32)
    image_ids = positions // IMG
    first_image = row_start // IMG
    chosen = jnp.zeros((local_rows,), jnp.int32)
    for image_slot_index in range(IMAGE_SLOTS):
        clamped = jnp.minimum(first_image + image_slot_index, images - 1)
        adapter_id = lax.dynamic_index_in_dim(adapter_of_image, clamped, 0, keepdims=False)
        chosen = jnp.where(image_ids == first_image + image_slot_index, adapter_id, chosen)
    column_ids = jnp.arange(ADAPTERS * RANK, dtype=jnp.int32) // RANK
    select = (column_ids[None, :] == chosen[:, None]).astype(jnp.float32)
    score_scale = HEAD_DIM ** (-0.5)
    ext_len = local_rows + 2 * (IMG - 1)
    w_qkv, w_out, w_fc1, w_fc2 = unpack(
        (
            lax.all_gather(qkv_weights, "dp", axis=0, tiled=True),
            lax.all_gather(out_weights, "dp", axis=0, tiled=True),
            lax.all_gather(fc1_weights, "dp", axis=0, tiled=True),
            lax.all_gather(fc2_weights, "dp", axis=0, tiled=True),
        )
    )
    tokens_f = tokens.astype(jnp.float32)
    normed1 = norm_rows(tokens_f, ln_gain[0], bias_model[0]).astype(jnp.bfloat16)
    shift_terms = (bias_model[1], jnp.zeros_like(bias_model[1]), bias_model[2])
    lowrank_qkv = []
    projected = []
    for part_id in range(3):
        lowrank = (select * product(normed1, qkv_down[part_id])).astype(jnp.bfloat16)
        lowrank_qkv.append(lowrank)
        projected.append(
            (
                product(normed1, w_qkv[part_id])
                + shift_terms[part_id]
                + product(lowrank, qkv_up[part_id])
            ).astype(jnp.bfloat16)
        )
    queries, key_rows, values = projected
    lower_keys = []
    lower_values = []
    upper_keys = []
    upper_values = []
    for distance in range(1, REACH + 1):
        rim_rows = min(local_rows, IMG - 1 - (distance - 1) * local_rows)
        from_below = shifted(
            (key_rows[local_rows - rim_rows :], values[local_rows - rim_rows :]), "dp", distance
        )
        from_above = shifted((key_rows[:rim_rows], values[:rim_rows]), "dp", -distance)
        lower_keys.insert(0, from_below[0])
        lower_values.insert(0, from_below[1])
        upper_keys.append(from_above[0])
        upper_values.append(from_above[1])
    ext_keys = jnp.concatenate(lower_keys + [key_rows] + upper_keys, axis=0).reshape(
        ext_len, HEADS, HEAD_DIM
    )
    ext_values = jnp.concatenate(lower_values + [values] + upper_values, axis=0).reshape(
        ext_len, HEADS, HEAD_DIM
    )
    query_heads = queries.reshape(local_rows, HEADS, HEAD_DIM)

    def slot_view(image_slot_index):
        image_id = first_image + image_slot_index
        offset = jnp.clip(image_id * IMG - row_start + IMG - 1, 0, ext_len - IMG)
        key_pos = row_start - (IMG - 1) + offset + jnp.arange(IMG, dtype=jnp.int32)
        key_ok = (key_pos >= 0) & (key_pos < all_tokens) & (key_pos // IMG == image_id)
        query_ok = (image_ids == image_id).astype(jnp.float32)
        slot_keys = lax.dynamic_slice_in_dim(ext_keys, offset, IMG, 0)
        slot_values = lax.dynamic_slice_in_dim(ext_values, offset, IMG, 0)
        raw_scores = (
            jnp.einsum("qhd,khd->hqk", query_heads, slot_keys, preferred_element_type=jnp.float32)
            * score_scale
        )
        scores = jnp.where(key_ok[None, None, :], raw_scores, -1e30)
        return (offset, query_ok, slot_keys, slot_values, scores)

    attended_f = jnp.zeros((local_rows, HEADS, HEAD_DIM), jnp.float32)
    log_totals = []
    for image_slot_index in range(IMAGE_SLOTS):
        offset, query_ok, slot_keys, slot_values, scores = slot_view(image_slot_index)
        row_max = jnp.max(scores, axis=-1, keepdims=True)
        log_total = row_max + jnp.log(jnp.sum(jnp.exp(scores - row_max), axis=-1, keepdims=True))
        log_totals.append(log_total)
        attn_probs = (jnp.exp(scores - log_total) * query_ok[None, :, None]).astype(jnp.bfloat16)
        attended_f = attended_f + jnp.einsum(
            "hqk,khd->qhd", attn_probs, slot_values, preferred_element_type=jnp.float32
        )
    attended = attended_f.reshape(local_rows, D).astype(jnp.bfloat16)
    lowrank_out = (select * product(attended, out_down)).astype(jnp.bfloat16)
    resid = tokens_f + product(attended, w_out) + bias_model[3] + product(lowrank_out, out_up)
    normed2 = norm_rows(resid, ln_gain[1], bias_model[4]).astype(jnp.bfloat16)
    lowrank_fc1 = (select * product(normed2, first_feedforward_down)).astype(jnp.bfloat16)
    pre_act = product(normed2, w_fc1) + first_feedforward_bias + product(lowrank_fc1, fc1_up)
    activated = gelu_tanh(pre_act).astype(jnp.bfloat16)
    lowrank_fc2 = (select * product(activated, fc2_down)).astype(jnp.bfloat16)
    output = (
        resid + product(activated, w_fc2) + bias_model[5] + product(lowrank_fc2, fc2_up)
    ).astype(jnp.bfloat16)
    back_qkv, back_out, back_fc1, back_fc2 = unpack(
        (
            lax.all_gather(qkv_weights, "dp", axis=0, tiled=True),
            lax.all_gather(out_weights, "dp", axis=0, tiled=True),
            lax.all_gather(fc1_weights, "dp", axis=0, tiled=True),
            lax.all_gather(fc2_weights, "dp", axis=0, tiled=True),
        )
    )
    grad_fc2_up = inner_product(lowrank_fc2, cotangent)
    glow_fc2 = (select * product_with_transpose(cotangent, fc2_up)).astype(jnp.bfloat16)
    grad_fc2_down = inner_product(activated, glow_fc2)
    grad_act = product_with_transpose(cotangent, back_fc2) + product_with_transpose(
        glow_fc2, fc2_down
    )
    gelu_back = jax.vjp(gelu_tanh, pre_act)[1]
    grad_pre = gelu_back(grad_act)[0].astype(jnp.bfloat16)
    grad_fc1_up = inner_product(lowrank_fc1, grad_pre)
    glow_fc1 = (select * product_with_transpose(grad_pre, fc1_up)).astype(jnp.bfloat16)
    grad_fc1_down = inner_product(normed2, glow_fc1)
    grad_norm2 = product_with_transpose(grad_pre, back_fc1) + product_with_transpose(
        glow_fc1, first_feedforward_down
    )
    second_norm_backward = jax.vjp(
        partial(norm_rows, gain_row=ln_gain[1], shift_row=bias_model[4]), resid
    )[1]
    residual_gradient = cotangent.astype(jnp.float32) + second_norm_backward(grad_norm2)[0]
    grad_branch = residual_gradient.astype(jnp.bfloat16)
    grad_out_up = inner_product(lowrank_out, grad_branch)
    glow_out = (select * product_with_transpose(grad_branch, out_up)).astype(jnp.bfloat16)
    grad_out_down = inner_product(attended, glow_out)
    grad_attended = (
        product_with_transpose(grad_branch, back_out) + product_with_transpose(glow_out, out_down)
    ).astype(jnp.bfloat16)
    grad_heads = grad_attended.reshape(local_rows, HEADS, HEAD_DIM)
    grad_queries = jnp.zeros((local_rows, HEADS, HEAD_DIM), jnp.float32)
    grad_ext_keys = jnp.zeros((ext_len, HEADS, HEAD_DIM), jnp.float32)
    grad_ext_values = jnp.zeros((ext_len, HEADS, HEAD_DIM), jnp.float32)
    for image_slot_index in range(IMAGE_SLOTS):
        offset, query_ok, slot_keys, slot_values, scores = slot_view(image_slot_index)
        probs_f = jnp.exp(scores - log_totals[image_slot_index]) * query_ok[None, :, None]
        probability_matrix = probs_f.astype(jnp.bfloat16)
        grad_probs = jnp.einsum(
            "qhd,khd->hqk", grad_heads, slot_values, preferred_element_type=jnp.float32
        )
        row_dot = jnp.sum(grad_probs * probs_f, axis=-1, keepdims=True)
        grad_scores = (probs_f * (grad_probs - row_dot)).astype(jnp.bfloat16)
        grad_queries = grad_queries + score_scale * jnp.einsum(
            "hqk,khd->qhd", grad_scores, slot_keys, preferred_element_type=jnp.float32
        )
        key_part = score_scale * jnp.einsum(
            "hqk,qhd->khd", grad_scores, query_heads, preferred_element_type=jnp.float32
        )
        value_part = jnp.einsum(
            "hqk,qhd->khd", probability_matrix, grad_heads, preferred_element_type=jnp.float32
        )
        grad_ext_keys = lax.dynamic_update_slice_in_dim(
            grad_ext_keys,
            lax.dynamic_slice_in_dim(grad_ext_keys, offset, IMG, 0) + key_part,
            offset,
            0,
        )
        grad_ext_values = lax.dynamic_update_slice_in_dim(
            grad_ext_values,
            lax.dynamic_slice_in_dim(grad_ext_values, offset, IMG, 0) + value_part,
            offset,
            0,
        )
    grad_ext_keys = grad_ext_keys.reshape(ext_len, D)
    grad_ext_values = grad_ext_values.reshape(ext_len, D)
    grad_keys_f = grad_ext_keys[IMG - 1 : IMG - 1 + local_rows]
    grad_values_f = grad_ext_values[IMG - 1 : IMG - 1 + local_rows]
    for distance in range(1, REACH + 1):
        rim_rows = min(local_rows, IMG - 1 - (distance - 1) * local_rows)
        low_begin = IMG - 1 - (distance - 1) * local_rows - rim_rows
        high_begin = IMG - 1 + distance * local_rows
        from_above = (
            shifted(
                grad_ext_keys[low_begin : low_begin + rim_rows].astype(jnp.bfloat16),
                "dp",
                -distance,
            ).astype(jnp.float32),
            shifted(
                grad_ext_values[low_begin : low_begin + rim_rows].astype(jnp.bfloat16),
                "dp",
                -distance,
            ).astype(jnp.float32),
        )
        from_below = (
            shifted(
                grad_ext_keys[high_begin : high_begin + rim_rows].astype(jnp.bfloat16),
                "dp",
                distance,
            ).astype(jnp.float32),
            shifted(
                grad_ext_values[high_begin : high_begin + rim_rows].astype(jnp.bfloat16),
                "dp",
                distance,
            ).astype(jnp.float32),
        )
        grad_keys_f = grad_keys_f.at[local_rows - rim_rows :].add(from_above[0])
        grad_values_f = grad_values_f.at[local_rows - rim_rows :].add(from_above[1])
        grad_keys_f = grad_keys_f.at[:rim_rows].add(from_below[0])
        grad_values_f = grad_values_f.at[:rim_rows].add(from_below[1])
    grad_parts = [
        grad_queries.reshape(local_rows, D).astype(jnp.bfloat16),
        grad_keys_f.astype(jnp.bfloat16),
        grad_values_f.astype(jnp.bfloat16),
    ]
    grad_norm1 = jnp.zeros((local_rows, D), jnp.float32)
    downs_list = []
    ups_list = []
    for part_id in range(3):
        grad_part = grad_parts[part_id]
        ups_list.append(inner_product(lowrank_qkv[part_id], grad_part))
        glow_part = (select * product_with_transpose(grad_part, qkv_up[part_id])).astype(
            jnp.bfloat16
        )
        downs_list.append(inner_product(normed1, glow_part))
        grad_norm1 = (
            grad_norm1
            + product_with_transpose(grad_part, back_qkv[part_id])
            + product_with_transpose(glow_part, qkv_down[part_id])
        )
    norm1_back = jax.vjp(
        partial(norm_rows, gain_row=ln_gain[0], shift_row=bias_model[0]), tokens_f
    )[1]
    grad_tokens = (residual_gradient + norm1_back(grad_norm1)[0]).astype(jnp.bfloat16)
    summed = (
        lax.psum_scatter(jnp.stack(downs_list).reshape(-1), "dp", scatter_dimension=0, tiled=True),
        lax.psum_scatter(jnp.stack(ups_list).reshape(-1), "dp", scatter_dimension=0, tiled=True),
        lax.psum_scatter(grad_out_down.reshape(-1), "dp", scatter_dimension=0, tiled=True),
        lax.psum_scatter(grad_out_up.reshape(-1), "dp", scatter_dimension=0, tiled=True),
        lax.psum_scatter(grad_fc1_down.reshape(-1), "dp", scatter_dimension=0, tiled=True),
        lax.psum_scatter(grad_fc1_up.reshape(-1), "dp", scatter_dimension=0, tiled=True),
        lax.psum_scatter(grad_fc2_down.reshape(-1), "dp", scatter_dimension=0, tiled=True),
        lax.psum_scatter(grad_fc2_up.reshape(-1), "dp", scatter_dimension=0, tiled=True),
    )
    return (
        output,
        grad_tokens,
        summed[0],
        summed[1],
        summed[2],
        summed[3],
        summed[4],
        summed[5],
        summed[6],
        summed[7],
    )


def solution(mesh):
    return jax.shard_map(
        local,
        mesh=mesh,
        in_specs=(
            P("dp", None),
            P("dp"),
            P("dp"),
            P("dp"),
            P("dp"),
            P(),
            P(),
            P(),
            P(),
            P(),
            P(),
            P(),
            P(),
            P(),
            P(),
            P(),
            P(),
            P("dp", None),
        ),
        out_specs=(
            P("dp", None),
            P("dp", None),
            P("dp"),
            P("dp"),
            P("dp"),
            P("dp"),
            P("dp"),
            P("dp"),
            P("dp"),
            P("dp"),
        ),
        check_vma=False,
    )
```

profile of v0, /device:TPU:0, one launch (start us, length us, event | category | flops | bytes accessed | tf_op | source)
XLA Modules:
  0.0 1444.3 jit_solution(840201771180181595)
XLA Ops:
  13.4 5.8 dynamic-update-slice.28
  23.6 5.8 dynamic-update-slice.29
  42.3 37.5 %all-gather.7.cloned.1.call-done = bf16[32,1,41472]{2,1,0:T(2,128)(2,1)} async-done(((bf16[1,1,41472]{2,1,0:T(2,128)(2,1)}), bf16[32,1,41472]{2,1,0:T(2,128)(2,1)}) %all-gather.7.cloned.1.call-update) | async-done | bytes 2654224 | tf_op jit(solution)/shard_map/all_gather | solution.py:107
  79.8 48.8 %reduce.37 = bf16[32,41472]{1,0:T(8,128)(2,1)} reduce(bf16[32,1,41472]{2,1,0:T(2,128)(2,1)} %all-gather.7.cloned.1.call-done, bf16[]{:T(256)} %constant.519), dimensions={1}, to_apply=%all-gather.1.reduce_sub_computation | reduce | bytes 5308418 | tf_op jit(solution)/shard_map/all_gather | solution.py:107
  128.6 6.5 reshape.582
  135.1 266.8 %all-reduce.17.cloned.1.call-done = (bf16[4958208]{0:T(1024)(128)(2,1)}, bf16[4958208]{0:T(1024)(128)(2,1)}) async-done(((bf16[4958208]{0:T(1024)(128)(2,1)}, bf16[4958208]{0:T(1024)(128)(2,1)}), (bf16[4958208]{0:T(1024)(128)(2,1)}, bf16[4958208]{0:T(1024)(128)(2,1)})) %all-reduce.17.cloned.1.call-update) | async-done | bytes 19832848
  401.8 20.1 %reshape.583 = bf16[1152,4304]{1,0:T(8,128)(2,1)} reshape(bf16[4958208]{0:T(1024)(128)(2,1)} %get-tuple-element.234) | data formatting | bytes 19832832 | tf_op jit(solution)/shard_map/reshape | solution.py:62
  422.0 19.3 %reshape.584 = bf16[4304,1152]{1,0:T(8,128)(2,1)} reshape(bf16[4958208]{0:T(1024)(128)(2,1)} %get-tuple-element.235) | data formatting | bytes 19832832 | tf_op jit(solution)/shard_map/reshape | solution.py:63
  441.2 9.1 convolution_bitcast_fusion.3
  450.3 66.3 %all-gather.5.cloned.1.call-done = bf16[32,1,124416]{2,1,0:T(2,128)(2,1)} async-done(((bf16[1,1,124416]{2,1,0:T(2,128)(2,1)}), bf16[32,1,124416]{2,1,0:T(2,128)(2,1)}) %all-gather.5.cloned.1.call-update) | async-done | bytes 7962640 | tf_op jit(solution)/shard_map/all_gather | solution.py:106
  516.6 167.5 %reduce.34 = bf16[32,124416]{1,0:T(8,128)(2,1)} reduce(bf16[32,1,124416]{2,1,0:T(2,128)(2,1)} %all-gather.5.cloned.1.call-done, bf16[]{:T(256)} %constant.519), dimensions={1}, to_apply=%all-gather.reduce_sub_computation | reduce | bytes 15925250 | tf_op jit(solution)/shard_map/all_gather | solution.py:106
  684.1 14.8 %reshape.599 = bf16[3981312]{0:T(1024)(128)(2,1)} reshape(bf16[32,124416]{1,0:T(8,128)(2,1)} %reduce.34) | data formatting | bytes 15925248
  698.9 5.6 fusion.145
  704.5 6.2 slice.382
  729.9 6.3 slice.377
  736.2 6.2 slice.370
  757.8 5.9 collective-permute-start.1
  765.5 5.4 collective-permute-start.2
  783.4 23.8 %collective-permute-done.11 = bf16[216,1152]{1,0:T(8,128)(2,1)S(1)} collective-permute-done((bf16[216,1152]{1,0:T(8,128)(2,1)S(1)}, bf16[216,1152]{1,0:T(8,128)(2,1)S(1)}, u32[]{:S(2)}, u32[]{:S(2)}) %collective-permute-start.11) | collective-permute-done | bytes 497696 | tf_op jit(solution)/shard_map/ppermute | solution.py:25
  809.5 6.4 copy.47
  815.9 4.9 fusion
  828.3 4.9 fusion.1
  847.8 6.4 copy.45
  854.2 8.4 fusion.10
  862.8 8.8 fusion.59
  874.5 6.7 convolution_add_fusion.2
  881.2 5.5 multiply_convert_fusion.2
  886.7 6.1 fusion.5
  901.8 9.5 fusion.25
  915.1 14.6 %dynamic_update_slice.14 = f32[1712,16,72]{0,2,1:T(8,128)} dynamic-update-slice(f32[1712,16,72]{0,2,1:T(8,128)} %broadcast.547.clone.1, f32[729,16,72]{0,2,1:T(8,128)} %fusion.25, s32[]{:T(128)S(6)} %min.17, s32[]{:T(128)} %constant.464.clone.1, s32[]{:T(128)} %constant.464.clone.1) | dynamic-update-slice | bytes 6718468 | tf_op jit(solution)/shard_map/dynamic_update_slice | solution.py:248
  929.8 10.8 bitcast_add_fusion
  940.6 14.3 dynamic_update_slice.15
  965.6 9.7 multiply_reduce_fusion.1
  975.4 7.2 multiply_reduce_fusion
  982.6 9.8 multiply_convert_fusion.1
  1000.1 14.7 %dynamic_update_slice.12 = f32[1712,16,72]{0,2,1:T(8,128)} dynamic-update-slice(f32[1712,16,72]{0,2,1:T(8,128)} %broadcast.547.clone, f32[729,16,72]{0,2,1:T(8,128)} %multiply_bitcast_fusion, s32[]{:T(128)S(6)} %min.17, s32[]{:T(128)} %constant.464.clone.1, s32[]{:T(128)} %constant.464.clone.1) | dynamic-update-slice | bytes 6718468 | tf_op jit(solution)/shard_map/dynamic_update_slice | solution.py:242
  1014.8 9.6 multiply_convert_fusion
  1027.0 6.0 bitcast_add_fusion.1
  1032.9 14.5 %dynamic_update_slice.13 = f32[1712,16,72]{0,2,1:T(8,128)} dynamic-update-slice(f32[1712,16,72]{0,2,1:T(8,128)} %dynamic_update_slice.12, f32[729,16,72]{0,2,1:T(8,128)} %bitcast_add_fusion.1, s32[]{:T(128)S(6)} %min.18, s32[]{:T(128)} %constant.464.clone.1, s32[]{:T(128)} %constant.464.clone.1) | dynamic-update-slice | bytes 6718468 | tf_op jit(solution)/shard_map/dynamic_update_slice | solution.py:242
  1080.5 14.5 %collective-permute-start.21 = (bf16[256,1152]{1,0:T(8,128)(2,1)}, bf16[256,1152]{1,0:T(8,128)(2,1)}, u32[]{:S(2)}, u32[]{:S(2)}) collective-permute-start(bf16[256,1152]{1,0:T(8,128)(2,1)} %copy.60), channel_id=1, source_target_pairs={{0,2},{1,3},{2,4},{3,5},{4,6},{5,7},{6,8},{7,9},{8,10},{9,11},{10,... | collective-permute-start | bytes 1769480 | tf_op jit(solution)/shard_map/ppermute | solution.py:25
  1114.5 4.7 fusion.64
  1136.6 6.5 collective-permute-start.23
  1150.7 4.7 collective-permute-start.15
  1159.0 13.6 collective-permute-start.17
  1174.4 17.7 %collective-permute-done.15 = bf16[256,1152]{1,0:T(8,128)(2,1)S(1)} collective-permute-done((bf16[256,1152]{1,0:T(8,128)(2,1)S(1)}, bf16[256,1152]{1,0:T(8,128)(2,1)S(1)}, u32[]{:S(2)}, u32[]{:S(2)}) %collective-permute-start.15) | collective-permute-done | bytes 589856 | tf_op jit(solution)/shard_map/ppermute | solution.py:25
  1192.5 11.5 collective-permute-done.16
  1213.5 7.4 fusion.19
  1230.5 195.1 %all-reduce.15.cloned.1.call-done = (f32[442368]{0:T(1024)}, f32[442368]{0:T(1024)}, f32[147456]{0:T(1024)}, f32[147456]{0:T(1024)}, f32[147456]{0:T(1024)}, /*i...) async-done(((f32[442368]{0:T(1024)}, f32[442368]{0:T(1024)}, f32[147456]{0:T(1024)}, f32[147456]{0:T(1024)}, f32[147456]{0:T(1024)}, /*index=5*/f32[550912]{0:T(1024)}, ...) | async-done | bytes 10305552
  (432 shorter events, 246.1 us)
Async XLA Ops:
  7.2 874.0 %copy-start = (bf16[128,4304]{0,1:T(8,128)(2,1)S(1)}, bf16[128,4304]{0,1:T(8,128)(2,1)}, u32[]{:S(2)}) copy-start(bf16[128,4304]{0,1:T(8,128)(2,1)} %param.71) | copy-start | bytes 3305476
  7.2 72.6 %all-gather.7.cloned.1.call-start = ((), (), s32[]{:S(2)}) async-start(), calls=%async_computation.1 | async-start | bytes 5474304 | tf_op jit(solution)/shard_map/all_gather | solution.py:107
  9.0 392.9 %all-reduce.17.cloned.1.call-start = ((), (), s32[]{:S(2)}) async-start(), calls=%async_computation.3 | async-start | bytes 39665664
  29.4 487.2 %all-gather.5.cloned.1.call-start = ((), (), s32[]{:S(2)}) async-start(), calls=%async_computation | async-start | bytes 16422912 | tf_op jit(solution)/shard_map/all_gather | solution.py:106
  31.4 1394.2 %all-reduce.15.cloned.1.call-start = ((), (), s32[]{:S(2)}) async-start(), calls=%async_computation.2 | async-start | bytes 20611072
  33.3 787.6 %copy-start.96 = (pred[729]{0:T(1024)(128)(4,1)}, pred[729]{0:T(1024)(128)(4,1)S(1)}, u32[]{:S(2)}) copy-start(pred[729]{0:T(1024)(128)(4,1)S(1)} %fusion.120) | copy-start | bytes 2191
  33.3 802.9 %copy-start.93 = (pred[729]{0:T(1024)(128)(4,1)}, pred[729]{0:T(1024)(128)(4,1)S(1)}, u32[]{:S(2)}) copy-start(pred[729]{0:T(1024)(128)(4,1)S(1)} %fusion.119) | copy-start | bytes 2191
  35.8 92.8 %copy-start.100 = (f32[256]{0:T(256)}, f32[256]{0:T(256)S(1)}, u32[]{:S(2)}) copy-start(f32[256]{0:T(256)S(1)} %fusion.133) | copy-start | bytes 3076
  36.6 713.6 %copy-start.19 = (bf16[256,1152]{1,0:T(8,128)(2,1)}, bf16[256,1152]{1,0:T(8,128)(2,1)S(1)}, u32[]{:S(2)}) copy-start(bf16[256,1152]{1,0:T(8,128)(2,1)S(1)} %fusion.70) | copy-start | bytes 1769476
  38.1 675.4 %copy-start.74 = (bf16[256,128]{1,0:T(8,128)(2,1)}, bf16[256,128]{1,0:T(8,128)(2,1)S(1)}, u32[]{:S(2)}) copy-start(bf16[256,128]{1,0:T(8,128)(2,1)S(1)} %fusion.76) | copy-start | bytes 196612
  41.4 703.9 %copy-start.76 = (bf16[256,128]{1,0:T(8,128)(2,1)}, bf16[256,128]{1,0:T(8,128)(2,1)S(1)}, u32[]{:S(2)}) copy-start(bf16[256,128]{1,0:T(8,128)(2,1)S(1)} %fusion.74) | copy-start | bytes 196612
  717.8 47.7 %collective-permute-start.7 = (bf16[256,1152]{1,0:T(8,128)(2,1)}, bf16[256,1152]{1,0:T(8,128)(2,1)}, u32[]{:S(2)}, u32[]{:S(2)}) collective-permute-start(bf16[256,1152]{1,0:T(8,128)(2,1)} %fusion.22), channel_id=1, source_target_pairs={{0,2},{1,3},{2,4},{3,5},{4,6},{5,7},{6,8},{7,9},{8,10},{9,11},{10,... | collective-permute-start | bytes 1769480 | tf_op jit(solution)/shard_map/ppermute | solution.py:25
  722.0 50.8 %collective-permute-start.8 = (bf16[256,1152]{1,0:T(8,128)(2,1)}, bf16[256,1152]{1,0:T(8,128)(2,1)}, u32[]{:S(2)}, u32[]{:S(2)}) collective-permute-start(bf16[256,1152]{1,0:T(8,128)(2,1)} %fusion.22), channel_id=1, source_target_pairs={{0,1},{1,2},{2,3},{3,4},{4,5},{5,6},{6,7},{7,8},{8,9},{9,10},{10,1... | collective-permute-start | bytes 1769480 | tf_op jit(solution)/shard_map/ppermute | solution.py:25
  725.1 52.9 %collective-permute-start.9 = (bf16[256,1152]{1,0:T(8,128)(2,1)}, bf16[256,1152]{1,0:T(8,128)(2,1)}, u32[]{:S(2)}, u32[]{:S(2)}) collective-permute-start(bf16[256,1152]{1,0:T(8,128)(2,1)} %fusion.22), channel_id=1, source_target_pairs={{1,0},{2,1},{3,2},{4,3},{5,4},{6,5},{7,6},{8,7},{9,8},{10,9},{11,1... | collective-permute-start | bytes 1769480 | tf_op jit(solution)/shard_map/ppermute | solution.py:25
  726.4 27.4 %collective-permute-start.6 = (bf16[216,1152]{1,0:T(8,128)(2,1)}, bf16[216,1152]{1,0:T(8,128)(2,1)}, u32[]{:S(2)}, u32[]{:S(2)}) collective-permute-start(bf16[216,1152]{1,0:T(8,128)(2,1)} %get-tuple-element.254), channel_id=1, source_target_pairs={{0,3},{1,4},{2,5},{3,6},{4,7},{5,8},{6,9},{7,10},{8,11},{9,12},{10... | collective-permute-start | bytes 1493000 | tf_op jit(solution)/shard_map/ppermute | solution.py:25
  746.7 11.1 collective-permute-start
  753.7 24.3 %copy-start.67 = (bf16[216,1152]{1,0:T(8,128)(2,1)S(1)}, bf16[216,1152]{1,0:T(8,128)(2,1)}, u32[]{:S(2)}) copy-start(bf16[216,1152]{1,0:T(8,128)(2,1)} %get-tuple-element.253) | copy-start | bytes 1492996
  753.8 27.5 %collective-permute-start.10 = (bf16[256,1152]{1,0:T(8,128)(2,1)}, bf16[256,1152]{1,0:T(8,128)(2,1)S(1)}, u32[]{:S(2)}, u32[]{:S(2)}) collective-permute-start(bf16[256,1152]{1,0:T(8,128)(2,1)} %fusion.22), channel_id=1, source_target_pairs={{2,0},{3,1},{4,2},{5,3},{6,4},{7,5},{8,6},{9,7},{10,8},{11,9},{12,... | collective-permute-start | bytes 1769480 | tf_op jit(solution)/shard_map/ppermute | solution.py:25
  757.8 75.4 %collective-permute-start.1 = (bf16[256,1152]{1,0:T(8,128)(2,1)S(1)}, bf16[256,1152]{1,0:T(8,128)(2,1)}, u32[]{:S(2)}, u32[]{:S(2)}) collective-permute-start(bf16[256,1152]{1,0:T(8,128)(2,1)S(1)} %fusion.20), channel_id=1, source_target_pairs={{0,2},{1,3},{2,4},{3,5},{4,6},{5,7},{6,8},{7,9},{8,10},{9,11},{10,... | collective-permute-start | bytes 1769480 | tf_op jit(solution)/shard_map/ppermute | solution.py:25
  765.5 73.7 %collective-permute-start.2 = (bf16[256,1152]{1,0:T(8,128)(2,1)S(1)}, bf16[256,1152]{1,0:T(8,128)(2,1)}, u32[]{:S(2)}, u32[]{:S(2)}) collective-permute-start(bf16[256,1152]{1,0:T(8,128)(2,1)S(1)} %fusion.20), channel_id=1, source_target_pairs={{0,1},{1,2},{2,3},{3,4},{4,5},{5,6},{6,7},{7,8},{8,9},{9,10},{10,1... | collective-permute-start | bytes 1769480 | tf_op jit(solution)/shard_map/ppermute | solution.py:25
  772.8 69.2 %collective-permute-start.3 = (bf16[256,1152]{1,0:T(8,128)(2,1)S(1)}, bf16[256,1152]{1,0:T(8,128)(2,1)}, u32[]{:S(2)}, u32[]{:S(2)}) collective-permute-start(bf16[256,1152]{1,0:T(8,128)(2,1)S(1)} %fusion.20), channel_id=1, source_target_pairs={{1,0},{2,1},{3,2},{4,3},{5,4},{6,5},{7,6},{8,7},{9,8},{10,9},{11,1... | collective-permute-start | bytes 1769480 | tf_op jit(solution)/shard_map/ppermute | solution.py:25
  778.0 29.2 %collective-permute-start.11 = (bf16[216,1152]{1,0:T(8,128)(2,1)S(1)}, bf16[216,1152]{1,0:T(8,128)(2,1)S(1)}, u32[]{:S(2)}, u32[]{:S(2)}) collective-permute-start(bf16[216,1152]{1,0:T(8,128)(2,1)S(1)} %copy-done.67), channel_id=1, source_target_pairs={{3,0},{4,1},{5,2},{6,3},{7,4},{8,5},{9,6},{10,7},{11,8},{12,9},{13... | collective-permute-start | bytes 1493000 | tf_op jit(solution)/shard_map/ppermute | solution.py:25
  781.3 62.8 %collective-permute-start.4 = (bf16[256,1152]{1,0:T(8,128)(2,1)S(1)}, bf16[256,1152]{1,0:T(8,128)(2,1)}, u32[]{:S(2)}, u32[]{:S(2)}) collective-permute-start(bf16[256,1152]{1,0:T(8,128)(2,1)S(1)} %fusion.20), channel_id=1, source_target_pairs={{2,0},{3,1},{4,2},{5,3},{6,4},{7,5},{8,6},{9,7},{10,8},{11,9},{12,... | collective-permute-start | bytes 1769480 | tf_op jit(solution)/shard_map/ppermute | solution.py:25
  807.2 38.7 %collective-permute-start.5 = (bf16[216,1152]{1,0:T(8,128)(2,1)}, bf16[216,1152]{1,0:T(8,128)(2,1)}, u32[]{:S(2)}, u32[]{:S(2)}) collective-permute-start(bf16[216,1152]{1,0:T(8,128)(2,1)} %get-tuple-element.255), channel_id=1, source_target_pairs={{3,0},{4,1},{5,2},{6,3},{7,4},{8,5},{9,6},{10,7},{11,8},{12,9},{13... | collective-permute-start | bytes 1493000 | tf_op jit(solution)/shard_map/ppermute | solution.py:25
  841.1 21.6 %copy-start.81 = (f32[16,256]{1,0:T(8,128)}, f32[16,256]{1,0:T(8,128)S(1)}, u32[]{:S(2)}) copy-start(f32[16,256]{1,0:T(8,128)S(1)} %log_add_fusion.1) | copy-start | bytes 49156
  873.5 24.1 %copy-start.7 = (f32[256,1152]{1,0:T(8,128)}, f32[256,1152]{1,0:T(8,128)S(1)}, u32[]{:S(2)}) copy-start(f32[256,1152]{1,0:T(8,128)S(1)} %get-tuple-element.264) | copy-start | bytes 3538948
  915.1 14.7 %copy-start.95 = (pred[729]{0:T(1024)(128)(4,1)S(1)}, pred[729]{0:T(1024)(128)(4,1)}, u32[]{:S(2)}) copy-start(pred[729]{0:T(1024)(128)(4,1)} %copy-done.93) | copy-start | bytes 2191
  915.1 14.7 %copy-start.103 = (f32[256]{0:T(256)S(1)}, f32[256]{0:T(256)}, u32[]{:S(2)}) copy-start(f32[256]{0:T(256)} %fusion.135) | copy-start | bytes 3076
  1032.9 25.1 %slice-start.3 = ((s8[6029312]{0:T(1024)(128)(4,1)}), s8[1835008]{0:T(1024)(128)(4,1)S(1)}, s32[]{:S(2)}) async-start(s8[6029312]{0:T(1024)(128)(4,1)} %bitcast.179), calls=%async_computation.7 | async-start | bytes 3670016
  1066.6 28.5 %copy-start.27 = (f32[256,16,72]{0,2,1:T(8,128)S(1)}, f32[256,16,72]{0,2,1:T(8,128)}, u32[]{:S(2)}) copy-start(f32[256,16,72]{0,2,1:T(8,128)} %slice.427) | copy-start | bytes 3538948
  1069.8 66.8 %collective-permute-start.18 = (bf16[256,1152]{1,0:T(8,128)(2,1)}, bf16[256,1152]{1,0:T(8,128)(2,1)}, u32[]{:S(2)}, u32[]{:S(2)}) collective-permute-start(bf16[256,1152]{1,0:T(8,128)(2,1)} %copy.56), channel_id=1, source_target_pairs={{1,0},{2,1},{3,2},{4,3},{5,4},{6,5},{7,6},{8,7},{9,8},{10,9},{11,1... | collective-permute-start | bytes 1769480 | tf_op jit(solution)/shard_map/ppermute | solution.py:25
  1073.2 69.8 %collective-permute-start.19 = (bf16[256,1152]{1,0:T(8,128)(2,1)}, bf16[256,1152]{1,0:T(8,128)(2,1)}, u32[]{:S(2)}, u32[]{:S(2)}) collective-permute-start(bf16[256,1152]{1,0:T(8,128)(2,1)} %copy.58), channel_id=1, source_target_pairs={{0,1},{1,2},{2,3},{3,4},{4,5},{5,6},{6,7},{7,8},{8,9},{9,10},{10,1... | collective-permute-start | bytes 1769480 | tf_op jit(solution)/shard_map/ppermute | solution.py:25
  1078.2 66.2 %collective-permute-start.20 = (bf16[256,1152]{1,0:T(8,128)(2,1)}, bf16[256,1152]{1,0:T(8,128)(2,1)}, u32[]{:S(2)}, u32[]{:S(2)}) collective-permute-start(bf16[256,1152]{1,0:T(8,128)(2,1)} %copy.59), channel_id=1, source_target_pairs={{2,0},{3,1},{4,2},{5,3},{6,4},{7,5},{8,6},{9,7},{10,8},{11,9},{12,... | collective-permute-start | bytes 1769480 | tf_op jit(solution)/shard_map/ppermute | solution.py:25
  1080.5 66.9 %collective-permute-start.21 = (bf16[256,1152]{1,0:T(8,128)(2,1)}, bf16[256,1152]{1,0:T(8,128)(2,1)}, u32[]{:S(2)}, u32[]{:S(2)}) collective-permute-start(bf16[256,1152]{1,0:T(8,128)(2,1)} %copy.60), channel_id=1, source_target_pairs={{0,2},{1,3},{2,4},{3,5},{4,6},{5,7},{6,8},{7,9},{8,10},{9,11},{10,... | collective-permute-start | bytes 1769480 | tf_op jit(solution)/shard_map/ppermute | solution.py:25
  1098.6 52.1 %collective-permute-start.22 = (bf16[216,1152]{1,0:T(8,128)(2,1)}, bf16[216,1152]{1,0:T(8,128)(2,1)}, u32[]{:S(2)}, u32[]{:S(2)}) collective-permute-start(bf16[216,1152]{1,0:T(8,128)(2,1)} %copy.61), channel_id=1, source_target_pairs={{3,0},{4,1},{5,2},{6,3},{7,4},{8,5},{9,6},{10,7},{11,8},{12,9},{13... | collective-permute-start | bytes 1493000 | tf_op jit(solution)/shard_map/ppermute | solution.py:25
  1134.4 14.3 copy-start.30
  1136.6 14.2 copy-start.60
  1136.6 20.1 %copy-start.65 = (bf16[216,1152]{1,0:T(8,128)(2,1)S(1)}, bf16[216,1152]{1,0:T(8,128)(2,1)}, u32[]{:S(2)}) copy-start(bf16[216,1152]{1,0:T(8,128)(2,1)} %copy.54) | copy-start | bytes 1492996
  1136.6 20.1 %collective-permute-start.23 = (bf16[216,1152]{1,0:T(8,128)(2,1)S(1)}, bf16[216,1152]{1,0:T(8,128)(2,1)S(1)}, u32[]{:S(2)}, u32[]{:S(2)}) collective-permute-start(bf16[216,1152]{1,0:T(8,128)(2,1)S(1)} %copy-done.66), channel_id=1, source_target_pairs={{0,3},{1,4},{2,5},{3,6},{4,7},{5,8},{6,9},{7,10},{8,11},{9,12},{10... | collective-permute-start | bytes 1493000 | tf_op jit(solution)/shard_map/ppermute | solution.py:25
  1143.1 15.9 %collective-permute-start.12 = (bf16[256,1152]{1,0:T(8,128)(2,1)S(1)}, bf16[256,1152]{1,0:T(8,128)(2,1)S(1)}, u32[]{:S(2)}, u32[]{:S(2)}) collective-permute-start(bf16[256,1152]{1,0:T(8,128)(2,1)S(1)} %copy-done.63), channel_id=1, source_target_pairs={{1,0},{2,1},{3,2},{4,3},{5,4},{6,5},{7,6},{8,7},{9,8},{10,9},{11,1... | collective-permute-start | bytes 1769480 | tf_op jit(solution)/shard_map/ppermute | solution.py:25
  1144.4 28.1 %collective-permute-start.13 = (bf16[256,1152]{1,0:T(8,128)(2,1)S(1)}, bf16[256,1152]{1,0:T(8,128)(2,1)S(1)}, u32[]{:S(2)}, u32[]{:S(2)}) collective-permute-start(bf16[256,1152]{1,0:T(8,128)(2,1)S(1)} %copy-done.62), channel_id=1, source_target_pairs={{0,1},{1,2},{2,3},{3,4},{4,5},{5,6},{6,7},{7,8},{8,9},{9,10},{10,1... | collective-permute-start | bytes 1769480 | tf_op jit(solution)/shard_map/ppermute | solution.py:25
  1147.5 27.0 %collective-permute-start.14 = (bf16[256,1152]{1,0:T(8,128)(2,1)S(1)}, bf16[256,1152]{1,0:T(8,128)(2,1)S(1)}, u32[]{:S(2)}, u32[]{:S(2)}) collective-permute-start(bf16[256,1152]{1,0:T(8,128)(2,1)S(1)} %copy-done.61), channel_id=1, source_target_pairs={{2,0},{3,1},{4,2},{5,3},{6,4},{7,5},{8,6},{9,7},{10,8},{11,9},{12,... | collective-permute-start | bytes 1769480 | tf_op jit(solution)/shard_map/ppermute | solution.py:25
  1150.7 41.4 %collective-permute-start.15 = (bf16[256,1152]{1,0:T(8,128)(2,1)S(1)}, bf16[256,1152]{1,0:T(8,128)(2,1)S(1)}, u32[]{:S(2)}, u32[]{:S(2)}) collective-permute-start(bf16[256,1152]{1,0:T(8,128)(2,1)S(1)} %copy-done.60), channel_id=1, source_target_pairs={{0,2},{1,3},{2,4},{3,5},{4,6},{5,7},{6,8},{7,9},{8,10},{9,11},{10,... | collective-permute-start | bytes 1769480 | tf_op jit(solution)/shard_map/ppermute | solution.py:25
  1156.7 35.5 %copy-start.29 = (f32[256,1152]{1,0:T(8,128)S(1)}, f32[256,1152]{1,0:T(8,128)}, u32[]{:S(2)}) copy-start(f32[256,1152]{1,0:T(8,128)} %copy.50) | copy-start | bytes 3538948
  1156.7 47.3 %collective-permute-start.16 = (bf16[216,1152]{1,0:T(8,128)(2,1)S(1)}, bf16[216,1152]{1,0:T(8,128)(2,1)S(1)}, u32[]{:S(2)}, u32[]{:S(2)}) collective-permute-start(bf16[216,1152]{1,0:T(8,128)(2,1)S(1)} %copy-done.65), channel_id=1, source_target_pairs={{3,0},{4,1},{5,2},{6,3},{7,4},{8,5},{9,6},{10,7},{11,8},{12,9},{13... | collective-permute-start | bytes 1493000 | tf_op jit(solution)/shard_map/ppermute | solution.py:25
  1158.3 34.2 %copy-start.8 = (f32[256,1152]{1,0:T(8,128)}, f32[256,1152]{1,0:T(8,128)S(1)}, u32[]{:S(2)}) copy-start(f32[256,1152]{1,0:T(8,128)S(1)} %fusion.84) | copy-start | bytes 3538948
  1159.0 45.3 %collective-permute-start.17 = (bf16[216,1152]{1,0:T(8,128)(2,1)S(1)}, bf16[216,1152]{1,0:T(8,128)(2,1)S(1)}, u32[]{:S(2)}, u32[]{:S(2)}) collective-permute-start(bf16[216,1152]{1,0:T(8,128)(2,1)S(1)} %copy-done.64), channel_id=1, source_target_pairs={{0,3},{1,4},{2,5},{3,6},{4,7},{5,8},{6,9},{7,10},{8,11},{9,12},{10... | collective-permute-start | bytes 1493000 | tf_op jit(solution)/shard_map/ppermute | solution.py:25
  1228.1 209.5 %copy-start.1 = (bf16[128,4304]{0,1:T(8,128)(2,1)S(1)}, bf16[128,4304]{0,1:T(8,128)(2,1)}, u32[]{:S(2)}) copy-start(bf16[128,4304]{0,1:T(8,128)(2,1)} %param.71) | copy-start | bytes 3305476
  (101 other events, 513.3 us)
Sparse Core Ops, SparseCore 0:
  11.5 68.2 all-gather.6
  86.2 315.5 all-reduce.16
  405.8 110.7 all-gather.4
  1212.9 212.6 all-reduce.14
where the time goes:
time: 1450 us; the launch traced here: 1440 us
  waiting for transfers between devices  622 us (43%)
  local copies, waits for them, and re-layouts  292 us (20%)
  other arithmetic  263 us (18%)
  matrix products  164 us (11%)
  starting transfers between devices  88.4 us (6%)
  between operations  15.8 us (1%)
    unnamed x6, waiting for transfers between devices  462 us
    all_gather x1, other arithmetic, local(): lax.all_gather(qkv_weights, 'dp', axis=0, tiled=True)  167 us
    ppermute x24, starting transfers between devices, shifted(): lax.ppermute(value, axis, [(source, source + steps) for source in range(f...  88.2 us
    unnamed x269, local copies, waits for them, and re-layouts  85.8 us
    all_gather x1, waiting for transfers between devices, local(): lax.all_gather(qkv_weights, 'dp', axis=0, tiled=True)  66.3 us
    ppermute x24, waiting for transfers between devices, shifted(): lax.ppermute(value, axis, [(source, source + steps) for source in range(f...  55.8 us
    all_gather x1, other arithmetic, local(): lax.all_gather(out_weights, 'dp', axis=0, tiled=True)  48.8 us
    dot_general x18, matrix products, product(): return jnp.dot(left, right, preferred_element_type=jnp.float32)  39.8 us
  transfers between devices with their start and end apart: 28, of which 9 were waited for; matrix products, arithmetic and copies ran while one was open for 18% of the time, Pallas kernels for 0%

commit v1 on v0

--- a/solution.py
+++ b/solution.py
@@ -1,14 +1,18 @@
+import functools
 from functools import partial
 
 import jax
 import jax.numpy as jnp
 from jax import lax
+from jax.experimental import pallas as pl
+from jax.experimental.pallas import tpu as pltpu
 from jax.sharding import PartitionSpec as P
 
 D = 1152
 HEADS = 16
 HEAD_DIM = 72
 FF = 4304
+FP = 4352
 IMG = 729
 RANK = 16
 ADAPTERS = 8
@@ -55,12 +59,265 @@
     )
 
 
-def unpack(flat):
+MESH = pl.DeviceIdType.MESH
+PLANE = 8
+STRIDE = 1
+ROWS = (216, 72, 72, 272)
+WIDE = (D, D, FP, D)
+TILES = tuple(rows // 8 for rows in ROWS)
+PIECES = (
+    (0, (0, 14), (14, 13)),
+    (1, (0, 5), (5, 4)),
+    (2, (0, 4), (4, 5)),
+    (3, (0, 17), (17, 17)),
+)
+
+
+def remote(src, dst, send, recv, to):
+    return pltpu.make_async_remote_copy(src_ref=src, dst_ref=dst, send_sem=send, recv_sem=recv, device_id=(to,), device_id_type=MESH)
+
+def gather_kernel(layers, qkv, out, fc1, fc2, o_qkv, o_out, o_fc1, o_fc2,
+                  h_qkv, h_out, h_fc1, h_fc2, ahead, ahead_in, wide, b_qkv, b_out, b_fc1, b_fc2,
+                  pair_send, pair_recv, ahead_sem, own_sem, z_send, hop_send, pair_out, ici_recv, pair_in):
+    me = lax.axis_index("dp")
+    core = lax.rem(me, 2)
+    x = lax.rem(me // 2, 2)
+    y = lax.rem(me // 4, 2)
+    z = me // PLANE
+    chip = me // 2
+    chips = 4 * layers
+    mate = me + 1 - 2 * core
+    to_x = me + 2 - 4 * x
+    to_y = me + 4 - 8 * y
+    barrier = pltpu.get_barrier_semaphore()
+    def greet(peer):
+        pl.semaphore_signal(barrier, inc=1, device_id=(peer,), device_id_type=MESH)
+    for peer in (mate, to_x, to_y):
+        greet(peer)
+    nxt = lax.rem(chip + 1, chips) * 2 + core
+    prv = lax.rem(chip + chips - 1, chips) * 2 + core
+    greet(nxt)
+    greet(prv)
+    spot_in_layer = lax.rem(me, PLANE)
+    greet(lax.rem(z + 1, layers) * PLANE + spot_in_layer)
+    greet(lax.rem(z + layers - 1, layers) * PLANE + spot_in_layer)
+    pl.semaphore_wait(barrier, 7)
+
+    ins = (qkv, out, fc1, fc2)
+    held = (h_qkv, h_out, h_fc1, h_fc2)
+    outs = (o_qkv, o_out, o_fc1, o_fc2)
+    blocks = (b_qkv, b_out, b_fc1, b_fc2)
+    for a in range(4):
+        remote(ins[a], held[a].at[core], pair_send.at[a], pair_recv.at[a], mate).start()
+        pltpu.make_async_copy(ins[a], held[a].at[core], own_sem.at[a]).start()
+
+    def pair_wait(a):
+        pltpu.make_async_copy(ins[a], held[a].at[core], own_sem.at[a]).wait()
+        remote(ins[a], held[a].at[1 - core], pair_send.at[a], pair_recv.at[a], mate).wait_recv()
+
+    def build(a):
+        half = ROWS[a] // 2
+        w = WIDE[a]
+        wide[0:half, 0:w] = held[a][0].astype(jnp.float32)
+        wide[half:2 * half, 0:w] = held[a][1].astype(jnp.float32)
+        blocks[a][...] = wide[0:2 * half, 0:w].reshape(half // 4, 8, w).astype(jnp.bfloat16)
+
+    def build_fc2():
+        wide[0:135, 0:D] = held[3][0].astype(jnp.float32)
+        lead = wide[134:135, 0:D] + held[3][1, 0:1].astype(jnp.float32)
+        wide[134:135, 0:D] = lead
+        wide[135:269, 0:D] = held[3][1].astype(jnp.float32)[1:135]
+        ahead[...] = wide[0:48, 0:D].astype(jnp.bfloat16)
+        remote(ahead, ahead_in, ahead_sem.at[0], ahead_sem.at[1], prv).start()
+    def finish_fc2():
+        remote(ahead, ahead_in, ahead_sem.at[0], ahead_sem.at[1], prv).wait_recv()
+        more = ahead_in[...].astype(jnp.float32)
+        wide[269:269 + 48, 0:D] = jnp.where(chip + 1 < chips, more, 0.0)
+        moved = pltpu.roll(wide[0:320, 0:D], 320 - 3 * chip, axis=0)[0:272]
+        b_fc2[...] = moved.reshape(34, 8, D).astype(jnp.bfloat16)
+
+    def spot(p, m, c):
+        a, *cuts = PIECES[p]
+        at, rows = cuts[c]
+        return outs[a].at[pl.ds(m * TILES[a] + at, rows)]
+
+    levels = [(d, s) for d in range(layers) for s in ((0,) if d == 0 else (-1, 1))]
+    plane = lax.rem(chip, 4)
+    corners = (plane, plane + 1 - 2 * x, plane + 2 - 4 * y, 3 - plane)
+
+    def there(d, s):
+        return (z - d >= 0) if s < 0 else (z + d < layers)
+
+    def also(yes, go):
+        if yes is None:
+            go()
+        else:
+            pl.when(yes)(go)
+
+    def level(d, s, go):
+        also(None if d == 0 else there(d, s), go)
+
+    def run(c):
+        def cut(p):
+            a, *cuts = PIECES[p]
+            return blocks[a].at[pl.ds(*cuts[c])]
+
+        def hops(p, src, m, slot, ways):
+            for w in ways:
+                if w == 2:
+                    remote(src, spot(p, m, c), pair_out.at[p, slot], pair_in.at[p, m], mate).start()
+                else:
+                    remote(src, spot(p, m, c), hop_send.at[p, slot, w], ici_recv.at[p, m], (to_x, to_y)[w]).start()
+
+        def along(p, src, m, slot, up, act):
+            def go():
+                d = remote(src, spot(p, m, c), z_send.at[p, slot, up], ici_recv.at[p, m], me + PLANE if up else me - PLANE)
+                act(d)
+            pl.when((z + 1 < layers) if up else (z > 0))(go)
+
+        def arrived(p, m):
+            s = spot(p, m, c)
+            pltpu.make_async_copy(s, s, ici_recv.at[p, m]).wait()
+            return s
+
+        start = lambda d: d.start()
+        finish = lambda d: d.wait_send()
+
+        def event(p, g, act):
+            n = len(levels)
+            if g == 0:
+                hops(p, cut(p), chip, 0, (0, 1))
+                for up in (0, 1):
+                    along(p, cut(p), chip, 0, up, start)
+            for i, (d, s) in enumerate(levels):
+                zz = z + s * d
+                if d >= 1 and d == g:
+                    def go():
+                        m = zz * 4 + corners[0]
+                        src = arrived(p, m)
+                        along(p, src, m, i, int(s < 0), start)
+                        hops(p, src, m, i, (0, 1, 2))
+                    level(d, s, go)
+                if d + 1 == g:
+                    def go():
+                        m = zz * 4 + corners[1]
+                        hops(p, arrived(p, m), m, n + i, (1, 2) if c == 0 else (2,))
+                        m = zz * 4 + corners[2]
+                        hops(p, arrived(p, m), m, 2 * n + i, (2,) if c == 0 else (0, 2))
+                    level(d, s, go)
+                if d + 2 == g:
+                    def go():
+                        m = zz * 4 + corners[3]
+                        hops(p, arrived(p, m), m, 3 * n + i, (2,))
+                    level(d, s, go)
+
+        launched = {0: 0, 1: 1, 2: 2, 3: 3}
+        made = -1
+        count = len(PIECES)
+        last = STRIDE * (count - 1) + layers + 1
+        for t in range(last + 1):
+            for p in range(count):
+                g = t - STRIDE * p
+                if 0 <= g <= layers + 1:
+                    a = PIECES[p][0]
+                    if g == 0 and a > made:
+                        made = a
+                        pair_wait(a)
+                        if a < 3:
+                            build(a)
+                        else:
+                            build_fc2()
+                            finish_fc2()
+                        pltpu.make_async_copy(blocks[a], outs[a].at[pl.ds(chip * TILES[a], TILES[a])], own_sem.at[a]).start()
+                    event(p, g, start)
+        for p in range(count):
+            for k in range(4):
+                for d, s in levels:
+                    if k == 0 and d == 0:
+                        continue
+                    def go():
+                        m = (z + s * d) * 4 + corners[k]
+                        q = spot(p, m, 1 - c)
+                        pltpu.make_async_copy(q, q, pair_in.at[p, m]).wait()
+                    level(d, s, go)
+        n = len(levels)
+        for p in range(count):
+            src = cut(p)
+            def sent(sem):
+                pltpu.make_async_copy(src, src, sem).wait()
+            for i, (d, s) in enumerate(levels):
+                def go():
+                    sent(hop_send.at[p, i, 0])
+                    sent(hop_send.at[p, i, 1])
+                    if c == 0:
+                        sent(hop_send.at[p, n + i, 1])
+                    else:
+                        sent(hop_send.at[p, 2 * n + i, 0])
+                    for k in range(4):
+                        if k or d:
+                            sent(pair_out.at[p, k * n + i])
+                    for up in (0, 1):
+                        if d == 0 or up == int(s < 0):
+                            pl.when((z + 1 < layers) if up else (z > 0))(lambda: sent(z_send.at[p, i, up]))
+                level(d, s, go)
+        for a in range(4):
+            remote(ins[a], held[a].at[core], pair_send.at[a], pair_recv.at[a], mate).wait_send()
+            pltpu.make_async_copy(blocks[a], outs[a].at[pl.ds(chip * TILES[a], TILES[a])], own_sem.at[a]).wait()
+        remote(ahead, ahead_in, ahead_sem.at[0], ahead_sem.at[1], prv).wait_send()
+
+    for c in (0, 1):
+        @pl.when(core == c)
+        def _():
+            run(c)
+
+def gather(n, qkv, out, fc1, fc2):
+    layers = n // PLANE
+    core = lax.rem(lax.axis_index("dp"), 2)
+    qkv = qkv.reshape(108, D)
+    out = out.reshape(36, D)
+    fc1 = jnp.pad(fc1.reshape(36, FF), ((0, 0), (0, FP - FF)))
+    half = jnp.zeros((576,), fc2.dtype)
+    fc2 = jnp.where(core == 0, jnp.concatenate([fc2, half]), jnp.concatenate([half, fc2])).reshape(135, D)
+    chips = 4 * layers
+    slots = 2 * layers - 1
+    count = len(PIECES)
+    dma = pltpu.SemaphoreType.DMA
+    return pl.pallas_call(
+        functools.partial(gather_kernel, layers),
+        out_shape=[jax.ShapeDtypeStruct((TILES[a] * chips, 8, WIDE[a]), jnp.bfloat16) for a in range(4)],
+        in_specs=[pl.BlockSpec(memory_space=pl.ANY)] * 4,
+        out_specs=[pl.BlockSpec(memory_space=pl.ANY)] * 4,
+        scratch_shapes=[
+            pltpu.VMEM((2, 108, D), jnp.bfloat16),
+            pltpu.VMEM((2, 36, D), jnp.bfloat16),
+            pltpu.VMEM((2, 36, FP), jnp.bfloat16),
+            pltpu.VMEM((2, 135, D), jnp.bfloat16),
+            pltpu.VMEM((48, D), jnp.bfloat16),
+            pltpu.VMEM((48, D), jnp.bfloat16),
+            pltpu.VMEM((320, FP), jnp.float32),
+            pltpu.VMEM((27, 8, D), jnp.bfloat16),
+            pltpu.VMEM((9, 8, D), jnp.bfloat16),
+            pltpu.VMEM((9, 8, FP), jnp.bfloat16),
+            pltpu.VMEM((34, 8, D), jnp.bfloat16),
+            dma((4,)), dma((4,)), dma((2,)), dma((4,)), dma((count, slots, 2)),
+            dma((count, 3 * slots, 2)), dma((count, 4 * slots)), dma((count, chips)), dma((count, chips)),
+        ],
+        compiler_params=pltpu.CompilerParams(collective_id=0, has_side_effects=True, vmem_limit_bytes=40 << 20),
+        name="gather_weights",
+    )(qkv, out, fc1, fc2)
+
+
+def frozen(qkv, out, fc1, fc2):
+    n = lax.axis_size("dp")
+    if n == 4 * PLANE:
+        w_qkv, w_out, w_fc1, w_fc2 = gather(n, qkv, out, fc1, fc2)
+        return (w_qkv.reshape(3, D, D), w_out.reshape(D, D), w_fc1.reshape(D, FP), w_fc2.reshape(FP, D))
+    qkv, out, fc1, fc2 = (lax.all_gather(v, "dp", axis=0, tiled=True) for v in (qkv, out, fc1, fc2))
     return (
-        flat[0].reshape(3, D, D),
-        flat[1].reshape(D, D),
-        flat[2].reshape(D, FF),
-        flat[3].reshape(FF, D),
+        qkv.reshape(3, D, D),
+        out.reshape(D, D),
+        jnp.pad(fc1.reshape(D, FF), ((0, 0), (0, FP - FF))),
+        jnp.pad(fc2.reshape(FF, D), ((0, FP - FF), (0, 0))),
     )
 
 
@@ -101,14 +358,11 @@
     select = (column_ids[None, :] == chosen[:, None]).astype(jnp.float32)
     score_scale = HEAD_DIM ** (-0.5)
     ext_len = local_rows + 2 * (IMG - 1)
-    w_qkv, w_out, w_fc1, w_fc2 = unpack(
-        (
-            lax.all_gather(qkv_weights, "dp", axis=0, tiled=True),
-            lax.all_gather(out_weights, "dp", axis=0, tiled=True),
-            lax.all_gather(fc1_weights, "dp", axis=0, tiled=True),
-            lax.all_gather(fc2_weights, "dp", axis=0, tiled=True),
-        )
-    )
+    w_qkv, w_out, w_fc1, w_fc2 = frozen(qkv_weights, out_weights, fc1_weights, fc2_weights)
+    tail = FP - FF
+    first_feedforward_bias = jnp.pad(first_feedforward_bias, (0, tail))
+    fc1_up = jnp.pad(fc1_up, ((0, 0), (0, tail)))
+    fc2_down = jnp.pad(fc2_down, ((0, tail), (0, 0)))
     tokens_f = tokens.astype(jnp.float32)
     normed1 = norm_rows(tokens_f, ln_gain[0], bias_model[0]).astype(jnp.bfloat16)
     shift_terms = (bias_model[1], jnp.zeros_like(bias_model[1]), bias_model[2])
@@ -184,14 +438,7 @@
     output = (
         resid + product(activated, w_fc2) + bias_model[5] + product(lowrank_fc2, fc2_up)
     ).astype(jnp.bfloat16)
-    back_qkv, back_out, back_fc1, back_fc2 = unpack(
-        (
-            lax.all_gather(qkv_weights, "dp", axis=0, tiled=True),
-            lax.all_gather(out_weights, "dp", axis=0, tiled=True),
-            lax.all_gather(fc1_weights, "dp", axis=0, tiled=True),
-            lax.all_gather(fc2_weights, "dp", axis=0, tiled=True),
-        )
-    )
+    back_qkv, back_out, back_fc1, back_fc2 = w_qkv, w_out, w_fc1, w_fc2
     grad_fc2_up = inner_product(lowrank_fc2, cotangent)
     glow_fc2 = (select * product_with_transpose(cotangent, fc2_up)).astype(jnp.bfloat16)
     grad_fc2_down = inner_product(activated, glow_fc2)
@@ -317,8 +564,8 @@
         lax.psum_scatter(grad_out_down.reshape(-1), "dp", scatter_dimension=0, tiled=True),
         lax.psum_scatter(grad_out_up.reshape(-1), "dp", scatter_dimension=0, tiled=True),
         lax.psum_scatter(grad_fc1_down.reshape(-1), "dp", scatter_dimension=0, tiled=True),
-        lax.psum_scatter(grad_fc1_up.reshape(-1), "dp", scatter_dimension=0, tiled=True),
-        lax.psum_scatter(grad_fc2_down.reshape(-1), "dp", scatter_dimension=0, tiled=True),
+        lax.psum_scatter(grad_fc1_up[:, :FF].reshape(-1), "dp", scatter_dimension=0, tiled=True),
+        lax.psum_scatter(grad_fc2_down[:FF].reshape(-1), "dp", scatter_dimension=0, tiled=True),
         lax.psum_scatter(grad_fc2_up.reshape(-1), "dp", scatter_dimension=0, tiled=True),
     )
     return (

time: 1450 us -> 911 us (0.63)
  waiting for transfers between devices: 622 us -> 277 us
  other arithmetic: 263 us -> 46.8 us
  Pallas kernels: 0 us -> 149 us
  local copies, waits for them, and re-layouts: 292 us -> 179 us
  starting transfers between devices: 88.4 us -> 68.8 us
    unnamed x6 -> x2, waiting for transfers between devices: 462 us -> 194 us
    all_gather x2 -> x0, other arithmetic: 216 us -> none  [the longest x1 167 us: local(): lax.all_gather(qkv_weights, 'dp', axis=0, tiled=True)]
    pallas_call x0 -> x1, Pallas kernels: none -> 149 us  [gather(): pl.pallas_call(functools.partial(gather_kernel, layers), out_shape=[jax.S...]
    all_gather x2 -> x0, waiting for transfers between devices: 104 us -> none  [the longest x1 66.3 us: local(): lax.all_gather(qkv_weights, 'dp', axis=0, tiled=True)]
    unnamed x269 -> x186, local copies, waits for them, and re-layouts: 85.8 us -> 34.3 us
    reshape x4 -> x5, local copies, waits for them, and re-layouts: 50.1 us -> 8.22 us  [the longest x1 4.18 us: local(): grad_fc1_up[:, :FF].reshape(-1)]
    ppermute x24, waiting for transfers between devices: 55.8 us -> 82.9 us  [shifted(): lax.ppermute(value, axis, [(source, source + steps) for source in range(f...]
    slice x4 -> x0, local copies, waits for them, and re-layouts: 24.4 us -> none  [local(): w_qkv[part_id]]
  transfers between devices with their start and end apart: 28 -> 25, of which waited for: 9 -> 8; matrix products, arithmetic and copies ran while one was open for 18% -> 13% of each run, Pallas kernels for 0% -> 0%
where the time goes in v1:
time: 911 us; the launch traced here: 899 us
  waiting for transfers between devices  277 us (30%)
  local copies, waits for them, and re-layouts  179 us (20%)
  matrix products  162 us (18%)
  Pallas kernels  149 us (16%)
  starting transfers between devices  68.8 us (8%)
  other arithmetic  46.8 us (5%)
  between operations  16.2 us (2%)
    unnamed x2, waiting for transfers between devices  194 us
    pallas_call x1, Pallas kernels, gather(): pl.pallas_call(functools.partial(gather_kernel, layers), out_shape=[jax.S...  149 us
    ppermute x24, waiting for transfers between devices, shifted(): lax.ppermute(value, axis, [(source, source + steps) for source in range(f...  82.9 us
    ppermute x24, starting transfers between devices, shifted(): lax.ppermute(value, axis, [(source, source + steps) for source in range(f...  68.8 us
    dot_general x18, matrix products, product_with_transpose(): lax.dot_general(left, right, (((1,), (1,)), ((), ())), preferred_element_...  35.8 us
    unnamed x186, local copies, waits for them, and re-layouts  34.3 us
    dynamic_update_slice x2, local copies, waits for them, and re-layouts, local(): lax.dynamic_update_slice_in_dim(grad_ext_keys, lax.dynamic_slice_in_dim(g...  29.1 us
    dynamic_update_slice x2, local copies, waits for them, and re-layouts, local(): lax.dynamic_update_slice_in_dim(grad_ext_values, lax.dynamic_slice_in_dim...  29 us
  transfers between devices with their start and end apart: 25, of which 8 were waited for; matrix products, arithmetic and copies ran while one was open for 13% of the time, Pallas kernels for 0%

profile of v1, /device:TPU:0, one launch (start us, length us, event | category | flops | bytes accessed | tf_op | source)
XLA Modules:
  0.0 898.8 jit_solution(1054535562950647047)
XLA Ops:
  18.3 149.2 %gather_weights.1 = (bf16[432,8,1152]{2,1,0:T(8,128)(2,1)S(1)}, bf16[144,8,1152]{2,1,0:T(8,128)(2,1)S(1)}, bf16[144,8,4352]{2,1,0:T(8,128)(2,1)}, bf16[544,8,1152]{2,1,0:T(8,128)(2,1)}) custom-call(bf16[108,1152]{1,0:T(8,128)(2,1)S(1)} %reshape.564.qkv, bf16[36,1152]{1,0:T(8,128)(2,1)S(1)} %reshape.565.out, bf16[36,4352]{1,0:T(8,128)(2,1)S(1)} %pad.50.fc1, ...), custom_call_target="tpu_custom_call" | custom-call | tf_op jit(solution)/shard_map/gather_weights/pallas_call | solution.py:285
  171.9 4.2 collective-permute-start.1
  181.9 3.6 collective-permute-start
  193.3 7.0 fusion.10
  202.0 4.2 collective-permute-done
  209.3 8.5 collective-permute-done.6
  221.0 4.7 collective-permute-start.8
  241.3 26.9 %collective-permute-done.5 = bf16[216,1152]{1,0:T(8,128)(2,1)S(1)} collective-permute-done((bf16[216,1152]{1,0:T(8,128)(2,1)S(1)}, bf16[216,1152]{1,0:T(8,128)(2,1)S(1)}, u32[]{:S(2)}, u32[]{:S(2)}) %collective-permute-start.5) | collective-permute-done | bytes 497696 | tf_op jit(solution)/shard_map/ppermute | solution.py:29
  269.1 6.4 copy.47
  282.2 6.4 copy.49
  288.6 4.9 fusion.9
  293.5 3.0 exponential_reduce_fusion
  296.5 5.8 fusion.8
  302.4 3.2 exponential_reduce_fusion.1
  305.6 6.0 fusion.24
  311.6 5.4 fusion.98
  319.9 3.1 fusion.13
  323.0 3.2 multiply_convert_fusion.2
  326.3 5.8 fusion.19
  332.1 7.7 fusion.4
  343.7 11.4 %multiply_reduce_fusion = (f32[16,256]{1,0:T(8,128)S(1)}, f32[16,256,729]{1,2,0:T(8,128)}) fusion(f32[256]{0:T(256)S(1)} %fusion.178, f32[16,256]{1,0:T(8,128)S(1)} %log_add_fusion, f32[16,256,729]{1,2,0:T(8,128)} %copy-done.5, pred[729]{0:T(1024)(128)(4,1)S(1)} %fusion.162, bf16[256,16,72]{0,2,1:T(8,128)(2,1)S(1)} %bitcast.214, ...), kind=kOutput, calls=%fused_computation.4 | convolution fusion | flops 447893504 | bytes 26396380 | tf_op jit(solution)/shard_map/qhd,khd->hqk/dot_general | solution.py:475
  355.2 11.8 %multiply_reduce_fusion.1 = (f32[16,256]{1,0:T(8,128)S(1)}, f32[16,256,729]{1,2,0:T(8,128)}) fusion(f32[256]{0:T(256)S(1)} %fusion.179, f32[16,256]{1,0:T(8,128)S(1)} %log_add_fusion.1, f32[16,256,729]{1,2,0:T(8,128)} %copy-done.6, pred[729]{0:T(1024)(128)(4,1)S(1)} %fusion.163, bf16[256,16,72]{0,2,1:T(8,128)(2,1)S(1)} %bitcast.215, ...), kind=kOutput, calls=%fused_computation.6 | convolution fusion | flops 447893504 | bytes 26396380 | tf_op jit(solution)/shard_map/qhd,khd->hqk/dot_general | solution.py:475
  367.0 6.9 multiply_convert_fusion
  374.0 5.4 fusion.73
  379.4 9.4 %multiply_convert_fusion.1 = bf16[16,256,729]{1,2,0:T(8,128)(2,1)S(1)} fusion(f32[16,256,729]{1,2,0:T(8,128)} %get-tuple-element.275, f32[16,256]{1,0:T(8,128)S(1)} %get-tuple-element.274, f32[256]{0:T(256)S(1)} %fusion.179, f32[16,256]{1,0:T(8,128)S(1)} %log_add_fusion.1, f32[16,256,729]{1,2,0:T(8,128)} %copy-done.6, pred[729]{0:T(1024)(128)(4,1)S(1)} %fusion.163), kind=kLoop, calls=%fused_computation.5 | loop fusion | flops 20901888 | bytes 29894360 | tf_op jit(solution)/shard_map/convert_element_type | solution.py:479
  388.9 3.8 multiply_bitcast_fusion
  392.6 3.8 broadcast.560.clone
  396.4 14.6 %dynamic_update_slice.12 = f32[1712,16,72]{0,2,1:T(8,128)} dynamic-update-slice(f32[1712,16,72]{0,2,1:T(8,128)} %broadcast.560.clone, f32[729,16,72]{0,2,1:T(8,128)} %multiply_bitcast_fusion, s32[]{:T(128)S(6)} %min.17, s32[]{:T(128)} %constant.470.clone.1, s32[]{:T(128)} %constant.470.clone.1) | dynamic-update-slice | bytes 6718468 | tf_op jit(solution)/shard_map/dynamic_update_slice | solution.py:489
  411.1 7.7 bitcast_add_fusion.1
  418.8 14.4 %dynamic_update_slice.13 = f32[1712,16,72]{0,2,1:T(8,128)} dynamic-update-slice(f32[1712,16,72]{0,2,1:T(8,128)} %dynamic_update_slice.12, f32[729,16,72]{0,2,1:T(8,128)} %bitcast_add_fusion.1, s32[]{:T(128)S(6)} %min.18, s32[]{:T(128)} %constant.470.clone.1, s32[]{:T(128)} %constant.470.clone.1) | dynamic-update-slice | bytes 6718468 | tf_op jit(solution)/shard_map/dynamic_update_slice | solution.py:489
  433.2 3.7 convert.16
  440.9 9.4 %fusion.64 = f32[729,16,72]{0,2,1:T(8,128)} fusion(bf16[256,16,72]{0,2,1:T(8,128)(2,1)S(1)} %bitcast.216, f32[16,256,729]{1,2,0:T(8,128)} %copy-done.6, f32[256]{0:T(256)S(1)} %fusion.179, f32[16,256]{1,0:T(8,128)S(1)} %log_add_fusion.1, pred[729]{0:T(1024)(128)(4,1)S(1)} %fusion.163), kind=kOutput, calls=%fused_computation.100 | convolution fusion | flops 444911616 | bytes 15911129 | tf_op jit(solution)/shard_map/hqk,qhd->khd/dot_general | solution.py:486
  450.3 3.8 broadcast.560.clone.1
  454.2 14.5 %dynamic_update_slice.14 = f32[1712,16,72]{0,2,1:T(8,128)} dynamic-update-slice(f32[1712,16,72]{0,2,1:T(8,128)} %broadcast.560.clone.1, f32[729,16,72]{0,2,1:T(8,128)} %fusion.64, s32[]{:T(128)S(6)} %min.17, s32[]{:T(128)} %constant.470.clone.1, s32[]{:T(128)} %constant.470.clone.1) | dynamic-update-slice | bytes 6718468 | tf_op jit(solution)/shard_map/dynamic_update_slice | solution.py:495
  468.6 10.8 %bitcast_add_fusion = f32[729,16,72]{0,2,1:T(8,128)} fusion(f32[1712,16,72]{0,2,1:T(8,128)} %dynamic_update_slice.14, s32[]{:T(128)S(6)} %min.18, bf16[256,16,72]{0,2,1:T(8,128)(2,1)S(1)} %bitcast.217, f32[16,256,729]{1,2,0:T(8,128)} %copy-done.5, f32[256]{0:T(256)S(1)} %fusion.178, f32[16,256]{1,0:T(8,128)S(1)} %log_add_fusion, pred[729]{0:T(1024)(128)(4,1)S(1)} %fusion.162), kind=kOutput, calls=%fused_computation.38 | convolution fusion | flops 445751424 | bytes 19270364 | tf_op jit(solution)/shard_map/hqk,qhd->khd/dot_general | solution.py:486
  479.4 14.6 %dynamic_update_slice.15 = f32[1712,16,72]{0,2,1:T(8,128)} dynamic-update-slice(f32[1712,16,72]{0,2,1:T(8,128)} %dynamic_update_slice.14, f32[729,16,72]{0,2,1:T(8,128)} %bitcast_add_fusion, s32[]{:T(128)S(6)} %min.18, s32[]{:T(128)} %constant.470.clone.1, s32[]{:T(128)} %constant.470.clone.1) | dynamic-update-slice | bytes 6718468 | tf_op jit(solution)/shard_map/dynamic_update_slice | solution.py:495
  494.0 3.9 convert.17
  513.5 5.6 collective-permute-start.21
  524.7 12.3 %collective-permute-start.19 = (bf16[256,1152]{1,0:T(8,128)(2,1)}, bf16[256,1152]{1,0:T(8,128)(2,1)}, u32[]{:S(2)}, u32[]{:S(2)}) collective-permute-start(bf16[256,1152]{1,0:T(8,128)(2,1)} %copy.61), channel_id=1, source_target_pairs={{0,1},{1,2},{2,3},{3,4},{4,5},{5,6},{6,7},{7,8},{8,9},{9,10},{10,1... | collective-permute-start | bytes 1769480 | tf_op jit(solution)/shard_map/ppermute | solution.py:29
  551.8 8.5 collective-permute-start.15
  580.3 4.2 reshape.580
  600.5 27.2 %collective-permute-done.22 = bf16[216,1152]{1,0:T(8,128)(2,1)S(1)} collective-permute-done((bf16[216,1152]{1,0:T(8,128)(2,1)S(1)}, bf16[216,1152]{1,0:T(8,128)(2,1)S(1)}, u32[]{:S(2)}, u32[]{:S(2)}) %collective-permute-start.22) | collective-permute-done | bytes 497696 | tf_op jit(solution)/shard_map/ppermute | solution.py:29
  629.3 6.2 collective-permute-done.23
  637.6 4.5 collective-permute-start.17
  643.5 6.6 collective-permute-done.16
  650.2 3.2 collective-permute-done.17
  663.9 7.9 fusion.36
  685.2 194.4 %all-reduce.17.cloned.1.call-done = (f32[442368]{0:T(1024)}, f32[442368]{0:T(1024)}, f32[147456]{0:T(1024)}, f32[147456]{0:T(1024)}, f32[147456]{0:T(1024)}, /*i...) async-done(((f32[442368]{0:T(1024)}, f32[442368]{0:T(1024)}, f32[147456]{0:T(1024)}, f32[147456]{0:T(1024)}, f32[147456]{0:T(1024)}, /*index=5*/f32[550912]{0:T(1024)}, ...) | async-done | bytes 10305552
  (340 shorter events, 182.8 us)
Async XLA Ops:
  7.2 312.3 %copy-start = (bf16[1152,128]{1,0:T(8,128)(2,1)S(1)}, bf16[1152,128]{1,0:T(8,128)(2,1)}, u32[]{:S(2)}) copy-start(bf16[1152,128]{1,0:T(8,128)(2,1)} %param.70) | copy-start | bytes 884740
  7.2 872.3 %all-reduce.17.cloned.1.call-start = ((), (), s32[]{:S(2)}) async-start(), calls=%async_computation | async-start | bytes 20611072
  8.6 158.9 %copy-start.61 = (f32[256]{0:T(256)}, f32[256]{0:T(256)S(1)}, u32[]{:S(2)}) copy-start(f32[256]{0:T(256)S(1)} %broadcast_multiply_fusion.1) | copy-start | bytes 3076
  10.0 160.0 %copy-start.65 = (f32[256]{0:T(256)}, f32[256]{0:T(256)S(1)}, u32[]{:S(2)}) copy-start(f32[256]{0:T(256)S(1)} %fusion.176) | copy-start | bytes 3076
  16.0 154.0 %copy-start.59 = (f32[1152]{0:T(1024)}, f32[1152]{0:T(1024)S(1)}, u32[]{:S(2)}) copy-start(f32[1152]{0:T(1024)S(1)} %get-tuple-element.278) | copy-start | bytes 13828
  18.3 172.7 %copy-start.15 = (bf16[256,1152]{1,0:T(8,128)(2,1)}, bf16[256,1152]{1,0:T(8,128)(2,1)S(1)}, u32[]{:S(2)}) copy-start(bf16[256,1152]{1,0:T(8,128)(2,1)S(1)} %fusion.109) | copy-start | bytes 1769476
  18.3 151.7 %copy-start.43 = (bf16[3,1152,128]{2,1,0:T(8,128)(2,1)S(1)}, bf16[3,1152,128]{2,1,0:T(8,128)(2,1)}, u32[]{:S(2)}) copy-start(bf16[3,1152,128]{2,1,0:T(8,128)(2,1)} %param.66) | copy-start | bytes 2654212
  168.9 22.1 %copy-start.2 = (bf16[432,8,1152]{2,1,0:T(8,128)(2,1)}, bf16[432,8,1152]{2,1,0:T(8,128)(2,1)S(1)}, u32[]{:S(2)}) copy-start(bf16[432,8,1152]{2,1,0:T(8,128)(2,1)S(1)} %get-tuple-element.222) | copy-start | bytes 23887876
  170.7 14.8 %copy-start.55 = (bf16[256,128]{1,0:T(8,128)(2,1)}, bf16[256,128]{1,0:T(8,128)(2,1)S(1)}, u32[]{:S(2)}) copy-start(bf16[256,128]{1,0:T(8,128)(2,1)S(1)} %fusion.113) | copy-start | bytes 196612
  170.7 22.5 %slice-start.5 = ((s8[10027008]{0:T(1024)(128)(4,1)}), s8[4194304]{0:T(1024)(128)(4,1)S(1)}, s32[]{:S(2)}) async-start(s8[10027008]{0:T(1024)(128)(4,1)} %bitcast.238), calls=%async_computation.6 | async-start | bytes 8388608
  171.9 49.1 %collective-permute-start.1 = (bf16[256,1152]{1,0:T(8,128)(2,1)}, bf16[256,1152]{1,0:T(8,128)(2,1)}, u32[]{:S(2)}, u32[]{:S(2)}) collective-permute-start(bf16[256,1152]{1,0:T(8,128)(2,1)} %fusion.50), channel_id=1, source_target_pairs={{0,2},{1,3},{2,4},{3,5},{4,6},{5,7},{6,8},{7,9},{8,10},{9,11},{10,... | collective-permute-start | bytes 1769480 | tf_op jit(solution)/shard_map/ppermute | solution.py:29
  176.0 51.6 %collective-permute-start.2 = (bf16[256,1152]{1,0:T(8,128)(2,1)}, bf16[256,1152]{1,0:T(8,128)(2,1)}, u32[]{:S(2)}, u32[]{:S(2)}) collective-permute-start(bf16[256,1152]{1,0:T(8,128)(2,1)} %fusion.50), channel_id=1, source_target_pairs={{0,1},{1,2},{2,3},{3,4},{4,5},{5,6},{6,7},{7,8},{8,9},{9,10},{10,1... | collective-permute-start | bytes 1769480 | tf_op jit(solution)/shard_map/ppermute | solution.py:29
  178.4 54.4 %collective-permute-start.3 = (bf16[256,1152]{1,0:T(8,128)(2,1)}, bf16[256,1152]{1,0:T(8,128)(2,1)}, u32[]{:S(2)}, u32[]{:S(2)}) collective-permute-start(bf16[256,1152]{1,0:T(8,128)(2,1)} %fusion.50), channel_id=1, source_target_pairs={{1,0},{2,1},{3,2},{4,3},{5,4},{6,5},{7,6},{8,7},{9,8},{10,9},{11,1... | collective-permute-start | bytes 1769480 | tf_op jit(solution)/shard_map/ppermute | solution.py:29
  181.9 24.2 %collective-permute-start = (bf16[216,1152]{1,0:T(8,128)(2,1)}, bf16[216,1152]{1,0:T(8,128)(2,1)}, u32[]{:S(2)}, u32[]{:S(2)}) collective-permute-start(bf16[216,1152]{1,0:T(8,128)(2,1)} %get-tuple-element.259), channel_id=1, source_target_pairs={{0,3},{1,4},{2,5},{3,6},{4,7},{5,8},{6,9},{7,10},{8,11},{9,12},{10... | collective-permute-start | bytes 1493000 | tf_op jit(solution)/shard_map/ppermute | solution.py:29
  188.3 29.6 %collective-permute-start.6 = (bf16[216,1152]{1,0:T(8,128)(2,1)}, bf16[216,1152]{1,0:T(8,128)(2,1)}, u32[]{:S(2)}, u32[]{:S(2)}) collective-permute-start(bf16[216,1152]{1,0:T(8,128)(2,1)} %get-tuple-element.257), channel_id=1, source_target_pairs={{0,3},{1,4},{2,5},{3,6},{4,7},{5,8},{6,9},{7,10},{8,11},{9,12},{10... | collective-permute-start | bytes 1493000 | tf_op jit(solution)/shard_map/ppermute | solution.py:29
  206.1 30.0 %collective-permute-start.4 = (bf16[256,1152]{1,0:T(8,128)(2,1)}, bf16[256,1152]{1,0:T(8,128)(2,1)S(1)}, u32[]{:S(2)}, u32[]{:S(2)}) collective-permute-start(bf16[256,1152]{1,0:T(8,128)(2,1)} %fusion.50), channel_id=1, source_target_pairs={{2,0},{3,1},{4,2},{5,3},{6,4},{7,5},{8,6},{9,7},{10,8},{11,9},{12,... | collective-permute-start | bytes 1769480 | tf_op jit(solution)/shard_map/ppermute | solution.py:29
  209.3 26.8 %copy-start.52 = (bf16[216,1152]{1,0:T(8,128)(2,1)S(1)}, bf16[216,1152]{1,0:T(8,128)(2,1)}, u32[]{:S(2)}) copy-start(bf16[216,1152]{1,0:T(8,128)(2,1)} %get-tuple-element.258) | copy-start | bytes 1492996
  217.8 20.4 %collective-permute-start.7 = (bf16[256,1152]{1,0:T(8,128)(2,1)S(1)}, bf16[256,1152]{1,0:T(8,128)(2,1)S(1)}, u32[]{:S(2)}, u32[]{:S(2)}) collective-permute-start(bf16[256,1152]{1,0:T(8,128)(2,1)S(1)} %fusion.52), channel_id=1, source_target_pairs={{0,2},{1,3},{2,4},{3,5},{4,6},{5,7},{6,8},{7,9},{8,10},{9,11},{10,... | collective-permute-start | bytes 1769480 | tf_op jit(solution)/shard_map/ppermute | solution.py:29
  221.0 19.4 %collective-permute-start.8 = (bf16[256,1152]{1,0:T(8,128)(2,1)S(1)}, bf16[256,1152]{1,0:T(8,128)(2,1)S(1)}, u32[]{:S(2)}, u32[]{:S(2)}) collective-permute-start(bf16[256,1152]{1,0:T(8,128)(2,1)S(1)} %fusion.52), channel_id=1, source_target_pairs={{0,1},{1,2},{2,3},{3,4},{4,5},{5,6},{6,7},{7,8},{8,9},{9,10},{10,1... | collective-permute-start | bytes 1769480 | tf_op jit(solution)/shard_map/ppermute | solution.py:29
  227.7 48.7 %collective-permute-start.9 = (bf16[256,1152]{1,0:T(8,128)(2,1)S(1)}, bf16[256,1152]{1,0:T(8,128)(2,1)}, u32[]{:S(2)}, u32[]{:S(2)}) collective-permute-start(bf16[256,1152]{1,0:T(8,128)(2,1)S(1)} %fusion.52), channel_id=1, source_target_pairs={{1,0},{2,1},{3,2},{4,3},{5,4},{6,5},{7,6},{8,7},{9,8},{10,9},{11,1... | collective-permute-start | bytes 1769480 | tf_op jit(solution)/shard_map/ppermute | solution.py:29
  232.8 45.5 %collective-permute-start.10 = (bf16[256,1152]{1,0:T(8,128)(2,1)S(1)}, bf16[256,1152]{1,0:T(8,128)(2,1)}, u32[]{:S(2)}, u32[]{:S(2)}) collective-permute-start(bf16[256,1152]{1,0:T(8,128)(2,1)S(1)} %fusion.52), channel_id=1, source_target_pairs={{2,0},{3,1},{4,2},{5,3},{6,4},{7,5},{8,6},{9,7},{10,8},{11,9},{12,... | collective-permute-start | bytes 1769480 | tf_op jit(solution)/shard_map/ppermute | solution.py:29
  236.1 32.1 %collective-permute-start.5 = (bf16[216,1152]{1,0:T(8,128)(2,1)S(1)}, bf16[216,1152]{1,0:T(8,128)(2,1)S(1)}, u32[]{:S(2)}, u32[]{:S(2)}) collective-permute-start(bf16[216,1152]{1,0:T(8,128)(2,1)S(1)} %copy-done.52), channel_id=1, source_target_pairs={{3,0},{4,1},{5,2},{6,3},{7,4},{8,5},{9,6},{10,7},{11,8},{12,9},{13... | collective-permute-start | bytes 1493000 | tf_op jit(solution)/shard_map/ppermute | solution.py:29
  238.2 42.0 %collective-permute-start.11 = (bf16[216,1152]{1,0:T(8,128)(2,1)}, bf16[216,1152]{1,0:T(8,128)(2,1)}, u32[]{:S(2)}, u32[]{:S(2)}) collective-permute-start(bf16[216,1152]{1,0:T(8,128)(2,1)} %get-tuple-element.256), channel_id=1, source_target_pairs={{3,0},{4,1},{5,2},{6,3},{7,4},{8,5},{9,6},{10,7},{11,8},{12,9},{13... | collective-permute-start | bytes 1493000 | tf_op jit(solution)/shard_map/ppermute | solution.py:29
  293.5 12.1 %copy-start.5 = (f32[16,256,729]{1,2,0:T(8,128)}, f32[16,256,729]{1,2,0:T(8,128)S(1)}, u32[]{:S(2)}) copy-start(f32[16,256,729]{1,2,0:T(8,128)S(1)} %get-tuple-element.263) | copy-start | bytes 35831812
  318.9 22.2 %copy-start.9 = (f32[256,1152]{1,0:T(8,128)}, f32[256,1152]{1,0:T(8,128)S(1)}, u32[]{:S(2)}) copy-start(f32[256,1152]{1,0:T(8,128)S(1)} %get-tuple-element.267) | copy-start | bytes 3538948
  343.7 23.3 %slice-start = ((s8[12058624]{0:T(1024)(128)(4,1)}), s8[4194304]{0:T(1024)(128)(4,1)S(1)}, s32[]{:S(2)}) async-start(s8[12058624]{0:T(1024)(128)(4,1)} %bitcast.197), calls=%async_computation.1 | async-start | bytes 8388608
  343.7 23.3 %slice-start.1 = ((s8[12058624]{0:T(1024)(128)(4,1)}), s8[4194304]{0:T(1024)(128)(4,1)S(1)}, s32[]{:S(2)}) async-start(s8[12058624]{0:T(1024)(128)(4,1)} %bitcast.197), calls=%async_computation.2 | async-start | bytes 8388608
  355.2 11.9 %slice-start.2 = ((s8[12058624]{0:T(1024)(128)(4,1)}), s8[3670016]{0:T(1024)(128)(4,1)S(1)}, s32[]{:S(2)}) async-start(s8[12058624]{0:T(1024)(128)(4,1)} %bitcast.197), calls=%async_computation.3 | async-start | bytes 7340032
  479.4 22.4 %slice-start.3 = ((s8[6029312]{0:T(1024)(128)(4,1)}), s8[1835008]{0:T(1024)(128)(4,1)S(1)}, s32[]{:S(2)}) async-start(s8[6029312]{0:T(1024)(128)(4,1)} %bitcast.199), calls=%async_computation.4 | async-start | bytes 3670016
  513.5 78.4 %collective-permute-start.21 = (bf16[256,1152]{1,0:T(8,128)(2,1)}, bf16[256,1152]{1,0:T(8,128)(2,1)}, u32[]{:S(2)}, u32[]{:S(2)}) collective-permute-start(bf16[256,1152]{1,0:T(8,128)(2,1)} %copy.63), channel_id=1, source_target_pairs={{0,2},{1,3},{2,4},{3,5},{4,6},{5,7},{6,8},{7,9},{8,10},{9,11},{10,... | collective-permute-start | bytes 1769480 | tf_op jit(solution)/shard_map/ppermute | solution.py:29
  521.3 72.4 %collective-permute-start.20 = (bf16[256,1152]{1,0:T(8,128)(2,1)}, bf16[256,1152]{1,0:T(8,128)(2,1)}, u32[]{:S(2)}, u32[]{:S(2)}) collective-permute-start(bf16[256,1152]{1,0:T(8,128)(2,1)} %copy.62), channel_id=1, source_target_pairs={{2,0},{3,1},{4,2},{5,3},{6,4},{7,5},{8,6},{9,7},{10,8},{11,9},{12,... | collective-permute-start | bytes 1769480 | tf_op jit(solution)/shard_map/ppermute | solution.py:29
  524.7 71.2 %collective-permute-start.19 = (bf16[256,1152]{1,0:T(8,128)(2,1)}, bf16[256,1152]{1,0:T(8,128)(2,1)}, u32[]{:S(2)}, u32[]{:S(2)}) collective-permute-start(bf16[256,1152]{1,0:T(8,128)(2,1)} %copy.61), channel_id=1, source_target_pairs={{0,1},{1,2},{2,3},{3,4},{4,5},{5,6},{6,7},{7,8},{8,9},{9,10},{10,1... | collective-permute-start | bytes 1769480 | tf_op jit(solution)/shard_map/ppermute | solution.py:29
  539.2 58.0 %collective-permute-start.18 = (bf16[256,1152]{1,0:T(8,128)(2,1)}, bf16[256,1152]{1,0:T(8,128)(2,1)}, u32[]{:S(2)}, u32[]{:S(2)}) collective-permute-start(bf16[256,1152]{1,0:T(8,128)(2,1)} %copy.59), channel_id=1, source_target_pairs={{1,0},{2,1},{3,2},{4,3},{5,4},{6,5},{7,6},{8,7},{9,8},{10,9},{11,1... | collective-permute-start | bytes 1769480 | tf_op jit(solution)/shard_map/ppermute | solution.py:29
  549.6 17.7 %copy-start.31 = (bf16[256,16,72]{0,2,1:T(8,128)(2,1)S(1)}, bf16[256,16,72]{0,2,1:T(8,128)(2,1)}, u32[]{:S(2)}) copy-start(bf16[256,16,72]{0,2,1:T(8,128)(2,1)} %get-tuple-element.252) | copy-start | bytes 1769476
  551.8 85.8 %collective-permute-start.15 = (bf16[256,1152]{1,0:T(8,128)(2,1)}, bf16[256,1152]{1,0:T(8,128)(2,1)}, u32[]{:S(2)}, u32[]{:S(2)}) collective-permute-start(bf16[256,1152]{1,0:T(8,128)(2,1)} %copy.56), channel_id=1, source_target_pairs={{0,2},{1,3},{2,4},{3,5},{4,6},{5,7},{6,8},{7,9},{8,10},{9,11},{10,... | collective-permute-start | bytes 1769480 | tf_op jit(solution)/shard_map/ppermute | solution.py:29
  592.0 35.8 %copy-start.50 = (bf16[216,1152]{1,0:T(8,128)(2,1)S(1)}, bf16[216,1152]{1,0:T(8,128)(2,1)}, u32[]{:S(2)}) copy-start(bf16[216,1152]{1,0:T(8,128)(2,1)} %copy.65) | copy-start | bytes 1492996
  592.0 43.5 %copy-start.49 = (bf16[216,1152]{1,0:T(8,128)(2,1)S(1)}, bf16[216,1152]{1,0:T(8,128)(2,1)}, u32[]{:S(2)}) copy-start(bf16[216,1152]{1,0:T(8,128)(2,1)} %copy.57) | copy-start | bytes 1492996
  592.0 50.0 %collective-permute-start.14 = (bf16[256,1152]{1,0:T(8,128)(2,1)S(1)}, bf16[256,1152]{1,0:T(8,128)(2,1)S(1)}, u32[]{:S(2)}, u32[]{:S(2)}) collective-permute-start(bf16[256,1152]{1,0:T(8,128)(2,1)S(1)} %copy-done.47), channel_id=1, source_target_pairs={{2,0},{3,1},{4,2},{5,3},{6,4},{7,5},{8,6},{9,7},{10,8},{11,9},{12,... | collective-permute-start | bytes 1769480 | tf_op jit(solution)/shard_map/ppermute | solution.py:29
  593.7 48.3 %collective-permute-start.13 = (bf16[256,1152]{1,0:T(8,128)(2,1)S(1)}, bf16[256,1152]{1,0:T(8,128)(2,1)S(1)}, u32[]{:S(2)}, u32[]{:S(2)}) collective-permute-start(bf16[256,1152]{1,0:T(8,128)(2,1)S(1)} %copy-done.45), channel_id=1, source_target_pairs={{0,1},{1,2},{2,3},{3,4},{4,5},{5,6},{6,7},{7,8},{8,9},{9,10},{10,1... | collective-permute-start | bytes 1769480 | tf_op jit(solution)/shard_map/ppermute | solution.py:29
  595.9 46.2 %collective-permute-start.12 = (bf16[256,1152]{1,0:T(8,128)(2,1)S(1)}, bf16[256,1152]{1,0:T(8,128)(2,1)S(1)}, u32[]{:S(2)}, u32[]{:S(2)}) collective-permute-start(bf16[256,1152]{1,0:T(8,128)(2,1)S(1)} %copy-done.46), channel_id=1, source_target_pairs={{1,0},{2,1},{3,2},{4,3},{5,4},{6,5},{7,6},{8,7},{9,8},{10,9},{11,1... | collective-permute-start | bytes 1769480 | tf_op jit(solution)/shard_map/ppermute | solution.py:29
  597.2 30.5 %collective-permute-start.22 = (bf16[216,1152]{1,0:T(8,128)(2,1)S(1)}, bf16[216,1152]{1,0:T(8,128)(2,1)S(1)}, u32[]{:S(2)}, u32[]{:S(2)}) collective-permute-start(bf16[216,1152]{1,0:T(8,128)(2,1)S(1)} %copy-done.51), channel_id=1, source_target_pairs={{3,0},{4,1},{5,2},{6,3},{7,4},{8,5},{9,6},{10,7},{11,8},{12,9},{13... | collective-permute-start | bytes 1493000 | tf_op jit(solution)/shard_map/ppermute | solution.py:29
  600.5 36.4 %copy-start.56 = (bf16[256,128]{1,0:T(8,128)(2,1)S(1)}, bf16[256,128]{1,0:T(8,128)(2,1)}, u32[]{:S(2)}) copy-start(bf16[256,128]{1,0:T(8,128)(2,1)} %copy-done.55) | copy-start | bytes 196612
  600.5 36.7 %copy-start.28 = (bf16[3,128,1152]{2,1,0:T(8,128)(2,1)S(1)}, bf16[3,128,1152]{2,1,0:T(8,128)(2,1)}, u32[]{:S(2)}) copy-start(bf16[3,128,1152]{2,1,0:T(8,128)(2,1)} %param.67) | copy-start | bytes 2654212
  627.8 7.7 collective-permute-start.23
  629.3 12.8 %copy-start.25 = (f32[256,1152]{1,0:T(8,128)S(1)}, f32[256,1152]{1,0:T(8,128)}, u32[]{:S(2)}) copy-start(f32[256,1152]{1,0:T(8,128)} %copy.53) | copy-start | bytes 3538948
  635.4 14.6 %collective-permute-start.16 = (bf16[216,1152]{1,0:T(8,128)(2,1)S(1)}, bf16[216,1152]{1,0:T(8,128)(2,1)S(1)}, u32[]{:S(2)}, u32[]{:S(2)}) collective-permute-start(bf16[216,1152]{1,0:T(8,128)(2,1)S(1)} %copy-done.49), channel_id=1, source_target_pairs={{3,0},{4,1},{5,2},{6,3},{7,4},{8,5},{9,6},{10,7},{11,8},{12,9},{13... | collective-permute-start | bytes 1493000 | tf_op jit(solution)/shard_map/ppermute | solution.py:29
  637.6 15.9 %collective-permute-start.17 = (bf16[216,1152]{1,0:T(8,128)(2,1)S(1)}, bf16[216,1152]{1,0:T(8,128)(2,1)S(1)}, u32[]{:S(2)}, u32[]{:S(2)}) collective-permute-start(bf16[216,1152]{1,0:T(8,128)(2,1)S(1)} %copy-done.48), channel_id=1, source_target_pairs={{0,3},{1,4},{2,5},{3,6},{4,7},{5,8},{6,9},{7,10},{8,11},{9,12},{10... | collective-permute-start | bytes 1493000 | tf_op jit(solution)/shard_map/ppermute | solution.py:29
  683.0 208.5 %copy-start.1 = (bf16[1152,128]{1,0:T(8,128)(2,1)S(1)}, bf16[1152,128]{1,0:T(8,128)(2,1)}, u32[]{:S(2)}) copy-start(bf16[1152,128]{1,0:T(8,128)(2,1)} %param.70) | copy-start | bytes 884740
  (60 other events, 300.0 us)
Sparse Core Ops, SparseCore 0:
  663.3 216.1 all-reduce.16

commit v2 on v1

v2 whole, which is shorter than its diff:
```python
import functools

import jax
import jax.numpy as jnp
from jax import lax
from jax.experimental import pallas as pl
from jax.experimental.pallas import tpu as pltpu
from jax.sharding import PartitionSpec as P

D = 1152
HEADS = 16
HEAD_DIM = 72
FF = 4304
FP = 4352
IMG = 729
RANK = 16
ADAPTERS = 8
epsilon = 1e-06


MESH = pl.DeviceIdType.MESH
PLANE = 8
STRIDE = 1
ROWS = (216, 72, 72, 272)
WIDE = (D, D, FP, D)
TILES = tuple(rows // 8 for rows in ROWS)
PIECES = (
    (0, (0, 14), (14, 13)),
    (1, (0, 5), (5, 4)),
    (2, (0, 4), (4, 5)),
    (3, (0, 17), (17, 17)),
)


def remote(src, dst, send, recv, to):
    return pltpu.make_async_remote_copy(src_ref=src, dst_ref=dst, send_sem=send, recv_sem=recv, device_id=(to,), device_id_type=MESH)

def gather_kernel(layers, qkv, out, fc1, fc2, o_qkv, o_out, o_fc1, o_fc2,
                  h_qkv, h_out, h_fc1, h_fc2, ahead, ahead_in, wide, b_qkv, b_out, b_fc1, b_fc2,
                  pair_send, pair_recv, ahead_sem, own_sem, z_send, hop_send, pair_out, ici_recv, pair_in):
    me = lax.axis_index("dp")
    core = lax.rem(me, 2)
    x = lax.rem(me // 2, 2)
    y = lax.rem(me // 4, 2)
    z = me // PLANE
    chip = me // 2
    chips = 4 * layers
    mate = me + 1 - 2 * core
    to_x = me + 2 - 4 * x
    to_y = me + 4 - 8 * y
    barrier = pltpu.get_barrier_semaphore()
    def greet(peer):
        pl.semaphore_signal(barrier, inc=1, device_id=(peer,), device_id_type=MESH)
    for peer in (mate, to_x, to_y):
        greet(peer)
    nxt = lax.rem(chip + 1, chips) * 2 + core
    prv = lax.rem(chip + chips - 1, chips) * 2 + core
    greet(nxt)
    greet(prv)
    spot_in_layer = lax.rem(me, PLANE)
    greet(lax.rem(z + 1, layers) * PLANE + spot_in_layer)
    greet(lax.rem(z + layers - 1, layers) * PLANE + spot_in_layer)
    pl.semaphore_wait(barrier, 7)

    ins = (qkv, out, fc1, fc2)
    held = (h_qkv, h_out, h_fc1, h_fc2)
    outs = (o_qkv, o_out, o_fc1, o_fc2)
    blocks = (b_qkv, b_out, b_fc1, b_fc2)
    for a in range(4):
        remote(ins[a], held[a].at[core], pair_send.at[a], pair_recv.at[a], mate).start()
        pltpu.make_async_copy(ins[a], held[a].at[core], own_sem.at[a]).start()

    def pair_wait(a):
        pltpu.make_async_copy(ins[a], held[a].at[core], own_sem.at[a]).wait()
        remote(ins[a], held[a].at[1 - core], pair_send.at[a], pair_recv.at[a], mate).wait_recv()

    def build(a):
        half = ROWS[a] // 2
        w = WIDE[a]
        wide[0:half, 0:w] = held[a][0].astype(jnp.float32)
        wide[half:2 * half, 0:w] = held[a][1].astype(jnp.float32)
        blocks[a][...] = wide[0:2 * half, 0:w].reshape(half // 4, 8, w).astype(jnp.bfloat16)

    def build_fc2():
        wide[0:135, 0:D] = held[3][0].astype(jnp.float32)
        lead = wide[134:135, 0:D] + held[3][1, 0:1].astype(jnp.float32)
        wide[134:135, 0:D] = lead
        wide[135:269, 0:D] = held[3][1].astype(jnp.float32)[1:135]
        ahead[...] = wide[0:48, 0:D].astype(jnp.bfloat16)
        remote(ahead, ahead_in, ahead_sem.at[0], ahead_sem.at[1], prv).start()
    def finish_fc2():
        remote(ahead, ahead_in, ahead_sem.at[0], ahead_sem.at[1], prv).wait_recv()
        more = ahead_in[...].astype(jnp.float32)
        wide[269:269 + 48, 0:D] = jnp.where(chip + 1 < chips, more, 0.0)
        moved = pltpu.roll(wide[0:320, 0:D], 320 - 3 * chip, axis=0)[0:272]
        b_fc2[...] = moved.reshape(34, 8, D).astype(jnp.bfloat16)

    def spot(p, m, c):
        a, *cuts = PIECES[p]
        at, rows = cuts[c]
        return outs[a].at[pl.ds(m * TILES[a] + at, rows)]

    levels = [(d, s) for d in range(layers) for s in ((0,) if d == 0 else (-1, 1))]
    plane = lax.rem(chip, 4)
    corners = (plane, plane + 1 - 2 * x, plane + 2 - 4 * y, 3 - plane)

    def there(d, s):
        return (z - d >= 0) if s < 0 else (z + d < layers)

    def also(yes, go):
        if yes is None:
            go()
        else:
            pl.when(yes)(go)

    def level(d, s, go):
        also(None if d == 0 else there(d, s), go)

    def run(c):
        def cut(p):
            a, *cuts = PIECES[p]
            return blocks[a].at[pl.ds(*cuts[c])]

        def hops(p, src, m, slot, ways):
            for w in ways:
                if w == 2:
                    remote(src, spot(p, m, c), pair_out.at[p, slot], pair_in.at[p, m], mate).start()
                else:
                    remote(src, spot(p, m, c), hop_send.at[p, slot, w], ici_recv.at[p, m], (to_x, to_y)[w]).start()

        def along(p, src, m, slot, up, act):
            def go():
                d = remote(src, spot(p, m, c), z_send.at[p, slot, up], ici_recv.at[p, m], me + PLANE if up else me - PLANE)
                act(d)
            pl.when((z + 1 < layers) if up else (z > 0))(go)

        def arrived(p, m):
            s = spot(p, m, c)
            pltpu.make_async_copy(s, s, ici_recv.at[p, m]).wait()
            return s

        start = lambda d: d.start()
        finish = lambda d: d.wait_send()

        def event(p, g, act):
            n = len(levels)
            if g == 0:
                hops(p, cut(p), chip, 0, (0, 1))
                for up in (0, 1):
                    along(p, cut(p), chip, 0, up, start)
            for i, (d, s) in enumerate(levels):
                zz = z + s * d
                if d >= 1 and d == g:
                    def go():
                        m = zz * 4 + corners[0]
                        src = arrived(p, m)
                        along(p, src, m, i, int(s < 0), start)
                        hops(p, src, m, i, (0, 1, 2))
                    level(d, s, go)
                if d + 1 == g:
                    def go():
                        m = zz * 4 + corners[1]
                        hops(p, arrived(p, m), m, n + i, (1, 2) if c == 0 else (2,))
                        m = zz * 4 + corners[2]
                        hops(p, arrived(p, m), m, 2 * n + i, (2,) if c == 0 else (0, 2))
                    level(d, s, go)
                if d + 2 == g:
                    def go():
                        m = zz * 4 + corners[3]
                        hops(p, arrived(p, m), m, 3 * n + i, (2,))
                    level(d, s, go)

        launched = {0: 0, 1: 1, 2: 2, 3: 3}
        made = -1
        count = len(PIECES)
        last = STRIDE * (count - 1) + layers + 1
        for t in range(last + 1):
            for p in range(count):
                g = t - STRIDE * p
                if 0 <= g <= layers + 1:
                    a = PIECES[p][0]
                    if g == 0 and a > made:
                        made = a
                        pair_wait(a)
                        if a < 3:
                            build(a)
                        else:
                            build_fc2()
                            finish_fc2()
                        pltpu.make_async_copy(blocks[a], outs[a].at[pl.ds(chip * TILES[a], TILES[a])], own_sem.at[a]).start()
                    event(p, g, start)
        for p in range(count):
            for k in range(4):
                for d, s in levels:
                    if k == 0 and d == 0:
                        continue
                    def go():
                        m = (z + s * d) * 4 + corners[k]
                        q = spot(p, m, 1 - c)
                        pltpu.make_async_copy(q, q, pair_in.at[p, m]).wait()
                    level(d, s, go)
        n = len(levels)
        for p in range(count):
            src = cut(p)
            def sent(sem):
                pltpu.make_async_copy(src, src, sem).wait()
            for i, (d, s) in enumerate(levels):
                def go():
                    sent(hop_send.at[p, i, 0])
                    sent(hop_send.at[p, i, 1])
                    if c == 0:
                        sent(hop_send.at[p, n + i, 1])
                    else:
                        sent(hop_send.at[p, 2 * n + i, 0])
                    for k in range(4):
                        if k or d:
                            sent(pair_out.at[p, k * n + i])
                    for up in (0, 1):
                        if d == 0 or up == int(s < 0):
                            pl.when((z + 1 < layers) if up else (z > 0))(lambda: sent(z_send.at[p, i, up]))
                level(d, s, go)
        for a in range(4):
            remote(ins[a], held[a].at[core], pair_send.at[a], pair_recv.at[a], mate).wait_send()
            pltpu.make_async_copy(blocks[a], outs[a].at[pl.ds(chip * TILES[a], TILES[a])], own_sem.at[a]).wait()
        remote(ahead, ahead_in, ahead_sem.at[0], ahead_sem.at[1], prv).wait_send()

    for c in (0, 1):
        @pl.when(core == c)
        def _():
            run(c)

def gather(n, qkv, out, fc1, fc2):
    layers = n // PLANE
    core = lax.rem(lax.axis_index("dp"), 2)
    qkv = qkv.reshape(108, D)
    out = out.reshape(36, D)
    fc1 = jnp.pad(fc1.reshape(36, FF), ((0, 0), (0, FP - FF)))
    half = jnp.zeros((576,), fc2.dtype)
    fc2 = jnp.where(core == 0, jnp.concatenate([fc2, half]), jnp.concatenate([half, fc2])).reshape(135, D)
    chips = 4 * layers
    slots = 2 * layers - 1
    count = len(PIECES)
    dma = pltpu.SemaphoreType.DMA
    return pl.pallas_call(
        functools.partial(gather_kernel, layers),
        out_shape=[jax.ShapeDtypeStruct((TILES[a] * chips, 8, WIDE[a]), jnp.bfloat16) for a in range(4)],
        in_specs=[pl.BlockSpec(memory_space=pl.ANY)] * 4,
        out_specs=[pl.BlockSpec(memory_space=pl.ANY)] * 4,
        scratch_shapes=[
            pltpu.VMEM((2, 108, D), jnp.bfloat16),
            pltpu.VMEM((2, 36, D), jnp.bfloat16),
            pltpu.VMEM((2, 36, FP), jnp.bfloat16),
            pltpu.VMEM((2, 135, D), jnp.bfloat16),
            pltpu.VMEM((48, D), jnp.bfloat16),
            pltpu.VMEM((48, D), jnp.bfloat16),
            pltpu.VMEM((320, FP), jnp.float32),
            pltpu.VMEM((27, 8, D), jnp.bfloat16),
            pltpu.VMEM((9, 8, D), jnp.bfloat16),
            pltpu.VMEM((9, 8, FP), jnp.bfloat16),
            pltpu.VMEM((34, 8, D), jnp.bfloat16),
            dma((4,)), dma((4,)), dma((2,)), dma((4,)), dma((count, slots, 2)),
            dma((count, 3 * slots, 2)), dma((count, 4 * slots)), dma((count, chips)), dma((count, chips)),
        ],
        compiler_params=pltpu.CompilerParams(collective_id=0, has_side_effects=True, vmem_limit_bytes=40 << 20),
        name="gather_weights",
    )(qkv, out, fc1, fc2)


def frozen(qkv, out, fc1, fc2):
    n = lax.axis_size("dp")
    if n == 4 * PLANE:
        w_qkv, w_out, w_fc1, w_fc2 = gather(n, qkv, out, fc1, fc2)
        return (w_qkv.reshape(3, D, D), w_out.reshape(D, D), w_fc1.reshape(D, FP), w_fc2.reshape(FP, D))
    qkv, out, fc1, fc2 = (lax.all_gather(v, "dp", axis=0, tiled=True) for v in (qkv, out, fc1, fc2))
    return (
        qkv.reshape(3, D, D),
        out.reshape(D, D),
        jnp.pad(fc1.reshape(D, FF), ((0, 0), (0, FP - FF))),
        jnp.pad(fc2.reshape(FF, D), ((0, FP - FF), (0, 0))),
    )


ROWS_HERE = 256
SIDE = 3
SPAN = 2 * SIDE + 1
LANES = 128
COLS = 384
STEP = 256
LOG2E = 1.4426950408889634
HIDE = -1e30


def mm(left, right):
    return jnp.dot(left, right, preferred_element_type=jnp.float32)


def mm_t(left, right):
    return lax.dot_general(left, right, (((1,), (1,)), ((), ())), preferred_element_type=jnp.float32)


def t_mm(left, right):
    return lax.dot_general(left, right, (((0,), (0,)), ((), ())), preferred_element_type=jnp.float32)


def moments(rows):
    center = rows - jnp.mean(rows, axis=-1, keepdims=True)
    return center, lax.rsqrt(jnp.mean(center * center, axis=-1, keepdims=True) + epsilon)


def shares_image(low, high):
    return (low * ROWS_HERE + ROWS_HERE - 1) // IMG >= (high * ROWS_HERE) // IMG


def met(me, n, k):
    other = me + k
    inside = (other >= 0) & (other < n)
    low, high = (me, other) if k > 0 else (other, me)
    return inside & shares_image(low, high)


def reach(me, n):
    first = jnp.int32(SIDE)
    last = jnp.int32(SIDE)
    for k in range(1, SIDE + 1):
        first = first - met(me, n, -k).astype(jnp.int32)
        last = last + met(me, n, k).astype(jnp.int32)
    return first, last


def slots_of(place, me):
    first = (me * ROWS_HERE) // IMG
    edge = first * IMG
    inside = jnp.where(place < edge + IMG, 0, 1)
    return jnp.where((place >= edge) & (place < edge + 2 * IMG), inside, -1)


def chosen_columns(adapters, images, me, block):
    shape = (ROWS_HERE, LANES)
    place = (me + block - SIDE) * ROWS_HERE + lax.broadcasted_iota(jnp.int32, shape, 0)
    column = lax.broadcasted_iota(jnp.int32, shape, 1)
    first = (me * ROWS_HERE) // IMG
    second = jnp.minimum(first + 1, images - 1)
    adapter = jnp.where(slots_of(place, me) == 0, adapters[first], adapters[second])
    return ((column >= adapter * RANK) & (column < adapter * RANK + RANK)).astype(jnp.float32)


def same_image(me, keys_block, query_block):
    shape = (ROWS_HERE, ROWS_HERE)
    key = (me + keys_block - SIDE) * ROWS_HERE + lax.broadcasted_iota(jnp.int32, shape, 0)
    query = (me + query_block - SIDE) * ROWS_HERE + lax.broadcasted_iota(jnp.int32, shape, 1)
    one = slots_of(key, me)
    return jnp.where((one == slots_of(query, me)) & (one >= 0), 0.0, HIDE)


def forward_kernel(n, images, tokens, w_qkv, w_out, w_fc1, w_fc2, gain, bias, fbias, qkv_down, qkv_up, out_down, out_up,
                   ff_down, fc1_up, fc2_down, fc2_up, adapters,
                   output, normed1, low_qkv, qt, kv, lse, mixed_t, mixed, low_out, resid, normed2, low_fc1, pre, low_fc2,
                   xs, v_qkv, v_out, v_fc1, v_fc2, tmp, shade, acc, act, x_send, x_recv, w_sem, fc1_sem, fc2_sem):
    me = lax.axis_index("dp")
    pltpu.make_async_copy(w_qkv, v_qkv, w_sem.at[0]).start()
    pltpu.make_async_copy(w_out, v_out, w_sem.at[1]).start()
    near = [k for k in range(-SIDE, SIDE + 1) if k]
    barrier = pltpu.get_barrier_semaphore()
    total = jnp.int32(0)
    for k in near:
        yes = met(me, n, k)
        total = total + yes.astype(jnp.int32)

        @pl.when(yes)
        def _():
            pl.semaphore_signal(barrier, inc=1, device_id=(me + k,), device_id_type=MESH)

    pl.semaphore_wait(barrier, total)

    def shift(i, k):
        return remote(tokens, xs.at[SIDE - k], x_send.at[i], x_recv.at[SIDE - k], me + k)

    for i, k in enumerate(near):
        @pl.when(met(me, n, k))
        def _():
            shift(i, k).start()
    xs[SIDE] = tokens[...]
    for i, k in enumerate(near):
        @pl.when(met(me, n, k))
        def _():
            pltpu.make_async_copy(xs.at[SIDE + k], xs.at[SIDE + k], x_recv.at[SIDE + k]).wait()
    begin, end = reach(me, n)

    pltpu.make_async_copy(w_qkv, v_qkv, w_sem.at[0]).wait()

    def project(j, carry):
        center, inv = moments(xs[j].astype(jnp.float32))
        n1 = (center * inv * gain[0:1] + bias[0:1]).astype(jnp.bfloat16)
        select = chosen_columns(adapters, images, me, j)
        @pl.when(j == SIDE)
        def _():
            normed1[...] = n1
        for p in range(3):
            low = (select * mm(n1, qkv_down[p])).astype(jnp.bfloat16)
            @pl.when(j == SIDE)
            def _():
                low_qkv[p] = low
            for c in range(0, D, COLS):
                y = mm(n1, v_qkv[p * D:(p + 1) * D, c:c + COLS]) + mm(low, qkv_up[p, :, c:c + COLS])
                if p != 1:
                    y = y + bias[(1, 0, 2)[p]:(1, 0, 2)[p] + 1, c:c + COLS]
                tmp[:, c:c + COLS] = y
            if p == 0:
                qt[j] = tmp[...].T.reshape(HEADS, HEAD_DIM, ROWS_HERE).astype(jnp.bfloat16)
            else:
                for h in range(HEADS):
                    kv[p - 1, j, h] = tmp[:, h * HEAD_DIM:(h + 1) * HEAD_DIM].astype(jnp.bfloat16)
        shade[j] = same_image(me, j, SIDE)
        return carry

    lax.fori_loop(begin, end + 1, project, 0)
    factor = HEAD_DIM ** (-0.5) * LOG2E

    def one_head(h, carry):
        q = qt[SIDE, h]

        def one_block(j, state):
            top, total, o = state
            s = mm(kv[0, j, h], q) * factor + shade[j]
            new = jnp.maximum(top, jnp.max(s, axis=0, keepdims=True))
            fade = jnp.exp2(top - new)
            p = jnp.exp2(s - new)
            total = total * fade + jnp.sum(p, axis=0, keepdims=True)
            o = o * fade + t_mm(kv[1, j, h], p.astype(jnp.bfloat16))
            return new, total, o

        start = (jnp.full((1, ROWS_HERE), HIDE, jnp.float32), jnp.zeros((1, ROWS_HERE), jnp.float32),
                 jnp.zeros((HEAD_DIM, ROWS_HERE), jnp.float32))
        top, total, o = lax.fori_loop(begin, end + 1, one_block, start)
        mixed_t[h] = o / total
        lse[h] = top + jnp.log2(total)
        return carry

    lax.fori_loop(0, HEADS, one_head, 0)
    att = mixed_t[...].reshape(D, ROWS_HERE).T.astype(jnp.bfloat16)
    mixed[...] = att
    select = chosen_columns(adapters, images, me, SIDE)
    pltpu.make_async_copy(w_out, v_out, w_sem.at[1]).wait()
    low = (select * mm(att, out_down[...])).astype(jnp.bfloat16)
    low_out[...] = low
    for c in range(0, D, COLS):
        s = slice(c, c + COLS)
        resid[:, s] = tokens[:, s].astype(jnp.float32) + mm(att, v_out[:, s]) + bias[3:4, s] + mm(low, out_up[:, s])
    center, inv = moments(resid[...])
    n2 = (center * inv * gain[1:2] + bias[4:5]).astype(jnp.bfloat16)
    normed2[...] = n2
    low1 = (select * mm(n2, ff_down[...])).astype(jnp.bfloat16)
    low_fc1[...] = low1

    def fetch1(i):
        slot = lax.rem(i, 2)
        cols = pl.ds(pl.multiple_of(i * STEP, STEP), STEP)
        return pltpu.make_async_copy(w_fc1.at[:, cols], v_fc1.at[slot], fc1_sem.at[slot])

    def fetch(i):
        slot = lax.rem(i, 2)
        rows = pl.ds(pl.multiple_of(i * STEP, STEP), STEP)
        return pltpu.make_async_copy(w_fc2.at[rows, :], v_fc2.at[slot], fc2_sem.at[slot])

    fetch1(0).start()
    fetch(0).start()
    acc[...] = jnp.zeros_like(acc)

    def feed(i, carry):
        @pl.when(i + 1 < FP // STEP)
        def _():
            fetch1(i + 1).start()
        fetch1(i).wait()
        s = pl.ds(pl.multiple_of(i * STEP, STEP), STEP)
        y = mm(n2, v_fc1[lax.rem(i, 2)]) + fbias[:, s] + mm(low1, fc1_up[:, s])
        pre[:, s] = y
        a = (0.5 * y * (1.0 + jnp.tanh(0.7978845608028654 * (y + 0.044715 * y * y * y)))).astype(jnp.bfloat16)
        act[:, s] = a
        acc[...] += mm(a, fc2_down[s, :])
        return carry

    lax.fori_loop(0, FP // STEP, feed, 0)
    low2 = (select * acc[...]).astype(jnp.bfloat16)
    low_fc2[...] = low2
    for c in range(0, D, COLS):
        s = slice(c, c + COLS)
        tmp[:, s] = resid[:, s] + bias[5:6, s] + mm(low2, fc2_up[:, s])

    def close(i, carry):
        @pl.when(i + 1 < FP // STEP)
        def _():
            fetch(i + 1).start()
        fetch(i).wait()
        s = pl.ds(pl.multiple_of(i * STEP, STEP), STEP)
        tmp[...] += mm(act[:, s], v_fc2[lax.rem(i, 2)])
        return carry

    lax.fori_loop(0, FP // STEP, close, 0)
    output[...] = tmp[...].astype(jnp.bfloat16)
    for i, k in enumerate(near):
        @pl.when(met(me, n, k))
        def _():
            shift(i, k).wait_send()


def forward(n, tokens, w_qkv, w_out, w_fc1, w_fc2, gain, bias, fbias, qkv_down, qkv_up, out_down, out_up, ff_down, fc1_up,
            fc2_down, fc2_up, adapters):
    bf, f32 = jnp.bfloat16, jnp.float32
    r = ROWS_HERE
    outs = [
        ((r, D), bf), ((r, D), bf), ((3, r, LANES), bf), ((SPAN, HEADS, HEAD_DIM, r), bf), ((2, SPAN, HEADS, r, HEAD_DIM), bf),
        ((HEADS, 1, r), f32), ((HEADS, HEAD_DIM, r), f32), ((r, D), bf), ((r, LANES), bf), ((r, D), f32), ((r, D), bf),
        ((r, LANES), bf), ((r, FP), f32), ((r, LANES), bf),
    ]
    vmem = pl.BlockSpec(memory_space=pltpu.VMEM)
    away = pl.BlockSpec(memory_space=pl.ANY)
    dma = pltpu.SemaphoreType.DMA
    return pl.pallas_call(
        functools.partial(forward_kernel, n, adapters.shape[0]),
        out_shape=[jax.ShapeDtypeStruct(*o) for o in outs],
        in_specs=[vmem] + [away] * 4 + [vmem] * 11 + [pl.BlockSpec(memory_space=pltpu.SMEM)],
        out_specs=[vmem] * len(outs),
        scratch_shapes=[
            pltpu.VMEM((SPAN, r, D), bf), pltpu.VMEM((3 * D, D), bf), pltpu.VMEM((D, D), bf), pltpu.VMEM((2, D, STEP), bf),
            pltpu.VMEM((2, STEP, D), bf), pltpu.VMEM((r, D), f32), pltpu.VMEM((SPAN, r, r), f32),
            pltpu.VMEM((r, LANES), f32), pltpu.VMEM((r, FP), bf), dma((6,)), dma((SPAN,)), dma((2,)), dma((2,)), dma((2,)),
        ],
        compiler_params=pltpu.CompilerParams(collective_id=1, has_side_effects=True, vmem_limit_bytes=63 << 20),
        name="layer_forward",
    )(tokens, w_qkv, w_out, w_fc1, w_fc2, gain, bias, fbias, qkv_down, qkv_up, out_down, out_up, ff_down, fc1_up, fc2_down,
      fc2_up, adapters)


def norm_back(center, inv, gain_row, grad):
    u = center * inv
    g = grad * gain_row
    return inv * (g - jnp.mean(g, axis=-1, keepdims=True) - u * jnp.mean(g * u, axis=-1, keepdims=True))


def backward_kernel(n, images, cotangent, tokens, w_qkv, w_out, w_fc1, w_fc2, gain, bias, qkv_down, qkv_up, out_down, out_up,
                    ff_down, fc1_up, fc2_down, fc2_up, adapters,
                    normed1, low_qkv, qt, kv, lse, mixed_t, mixed, low_out, resid, normed2, low_fc1, pre, low_fc2,
                    grad_tokens, g_qkv_down, g_qkv_up, g_out_down, g_out_up, g_ff_down, g_fc1_up, g_fc2_down, g_fc2_up,
                    v_qkv, v_out, v_fc1, v_fc2, v_kv, own_kv, wide, dres, acc, dat, stat, dq, dk, dv,
                    send, recv, w_sem, fc1_sem, fc2_sem, kv_sem):
    me = lax.axis_index("dp")
    own = pltpu.make_async_copy(kv.at[:, SIDE], own_kv, w_sem.at[0])
    own.start()
    get_out = pltpu.make_async_copy(w_out, v_out, w_sem.at[1])
    get_out.start()
    get_qkv = pltpu.make_async_copy(w_qkv, v_qkv, w_sem.at[2])
    get_qkv.start()

    def fetch1(i):
        slot = lax.rem(i, 2)
        cols = pl.ds(pl.multiple_of(i * STEP, STEP), STEP)
        return pltpu.make_async_copy(w_fc1.at[:, cols], v_fc1.at[slot], fc1_sem.at[slot])

    def fetch2(i):
        slot = lax.rem(i, 2)
        rows = pl.ds(pl.multiple_of(i * STEP, STEP), STEP)
        return pltpu.make_async_copy(w_fc2.at[rows, :], v_fc2.at[slot], fc2_sem.at[slot])

    fetch1(0).start()
    fetch2(0).start()
    near = [k for k in range(-SIDE, SIDE + 1) if k]
    barrier = pltpu.get_barrier_semaphore()
    total = jnp.int32(0)
    for k in near:
        yes = met(me, n, k)
        total = total + yes.astype(jnp.int32)

        @pl.when(yes)
        def _():
            pl.semaphore_signal(barrier, inc=1, device_id=(me + k,), device_id_type=MESH)

    begin, end = reach(me, n)
    bf = jnp.bfloat16
    select = chosen_columns(adapters, images, me, SIDE)
    e = cotangent[...]
    g_fc2_up[...] = t_mm(low_fc2[...], e)
    glow2 = (select * mm_t(e, fc2_up[...])).astype(bf)
    acc[...] = jnp.zeros_like(acc)
    wide[...] = jnp.zeros_like(wide)
    low1 = low_fc1[...]

    def feed(i, carry):
        @pl.when(i + 1 < FP // STEP)
        def _():
            fetch1(i + 1).start()
            fetch2(i + 1).start()
        fetch1(i).wait()
        fetch2(i).wait()
        slot = lax.rem(i, 2)
        s = pl.ds(pl.multiple_of(i * STEP, STEP), STEP)
        y = pre[:, s]
        t = jnp.tanh(0.7978845608028654 * (y + 0.044715 * y * y * y))
        half = 0.5 * (1.0 + t)
        a = (y * half).astype(bf)
        slope = half + 0.5 * y * (1.0 - t * t) * (0.7978845608028654 * (1.0 + 3.0 * 0.044715 * y * y))
        g_fc2_down[s, :] = t_mm(a, glow2)
        g = mm_t(e, v_fc2[slot]) + mm_t(glow2, fc2_down[s, :])
        gp = (g * slope).astype(bf)
        g_fc1_up[:, s] = t_mm(low1, gp)
        acc[...] += mm_t(gp, fc1_up[:, s])
        wide[...] += mm_t(gp, v_fc1[slot])
        return carry

    lax.fori_loop(0, FP // STEP, feed, 0)
    glow1 = (select * acc[...]).astype(bf)
    g_ff_down[...] = t_mm(normed2[...], glow1)
    center, inv = moments(resid[...])
    dres[...] = e.astype(jnp.float32) + norm_back(center, inv, gain[1:2], wide[...] + mm_t(glow1, ff_down[...]))
    gb = dres[...].astype(bf)
    g_out_up[...] = t_mm(low_out[...], gb)
    glow = (select * mm_t(gb, out_up[...])).astype(bf)
    g_out_down[...] = t_mm(mixed[...], glow)
    get_out.wait()
    for c in range(0, D, COLS):
        wide[:, c:c + COLS] = mm_t(gb, v_out[c:c + COLS, :]) + mm_t(glow, out_down[c:c + COLS, :])
    da = wide[...].T.reshape(HEADS, HEAD_DIM, ROWS_HERE).astype(bf)
    dat[SIDE] = da
    delta = jnp.sum(da.astype(jnp.float32) * mixed_t[...], axis=1, keepdims=True)
    stat[SIDE, :, 0:1, :] = lse[...]
    stat[SIDE, :, 1:2, :] = delta

    pl.semaphore_wait(barrier, total)

    def shift(i, k, what):
        ref = (dat, stat)[what]
        return remote(ref.at[SIDE], ref.at[SIDE - k], send.at[what, i], recv.at[what, SIDE - k], me + k)

    for i, k in enumerate(near):
        @pl.when(met(me, n, k))
        def _():
            shift(i, k, 0).start()
            shift(i, k, 1).start()

    factor = HEAD_DIM ** (-0.5) * LOG2E
    dq[...] = jnp.zeros_like(dq)

    def block(h, keys, vals, q, d, st, shade, which):
        s = mm(keys, q) * factor + shade
        p = jnp.exp2(s - st[0:1])
        ds = (p * (mm(vals, d) - st[1:2])).astype(bf)
        if which != 2:
            dq[h] += t_mm(keys, ds)
        if which == 0:
            dk[h] = mm_t(q, ds)
            dv[h] = mm_t(d, p.astype(bf))
        if which == 2:
            dk[h] += mm_t(q, ds)
            dv[h] += mm_t(d, p.astype(bf))

    own.wait()
    shade = same_image(me, SIDE, SIDE)

    def own_head(h, carry):
        block(h, own_kv[0, h], own_kv[1, h], qt[SIDE, h], dat[SIDE, h], stat[SIDE, h], shade, 0)
        return carry

    def get_kv(j):
        slot = lax.rem(j, 2)
        return pltpu.make_async_copy(kv.at[:, j], v_kv.at[slot], kv_sem.at[slot])

    get_kv(begin).start()
    lax.fori_loop(0, HEADS, own_head, 0)

    def pass_one(j, carry):
        @pl.when(j < end)
        def _():
            get_kv(j + 1).start()
        get_kv(j).wait()

        @pl.when(j != SIDE)
        def _():
            shade = same_image(me, j, SIDE)
            slot = lax.rem(j, 2)

            def head(h, carry):
                block(h, v_kv[slot, 0, h], v_kv[slot, 1, h], qt[SIDE, h], dat[SIDE, h], stat[SIDE, h], shade, 1)
                return carry

            lax.fori_loop(0, HEADS, head, 0)
        return carry

    lax.fori_loop(begin, end + 1, pass_one, 0)
    for i, k in enumerate(near):
        @pl.when(met(me, n, k))
        def _():
            for what, ref in enumerate((dat, stat)):
                pltpu.make_async_copy(ref.at[SIDE + k], ref.at[SIDE + k], recv.at[what, SIDE + k]).wait()

    def pass_two(j, carry):
        @pl.when(j != SIDE)
        def _():
            shade = same_image(me, SIDE, j)

            def head(h, carry):
                block(h, own_kv[0, h], own_kv[1, h], qt[j, h], dat[j, h], stat[j, h], shade, 2)
                return carry

            lax.fori_loop(0, HEADS, head, 0)
        return carry

    lax.fori_loop(begin, end + 1, pass_two, 0)
    get_qkv.wait()
    n1 = normed1[...]
    for p, source in enumerate((dq, dk, dv)):
        value = source[...] * HEAD_DIM ** (-0.5) if p < 2 else source[...]
        g = value.reshape(D, ROWS_HERE).T.astype(bf)
        g_qkv_up[p * LANES:(p + 1) * LANES, :] = t_mm(low_qkv[p], g)
        glow = (select * mm_t(g, qkv_up[p])).astype(bf)
        g_qkv_down[p * D:(p + 1) * D, :] = t_mm(n1, glow)
        for c in range(0, D, COLS):
            s = slice(c, c + COLS)
            y = mm_t(g, v_qkv[p * D + c:p * D + c + COLS, :]) + mm_t(glow, qkv_down[p, s, :])
            wide[:, s] = y if p == 0 else wide[:, s] + y
    center, inv = moments(tokens[...].astype(jnp.float32))
    grad_tokens[...] = (dres[...] + norm_back(center, inv, gain[0:1], wide[...])).astype(bf)
    for i, k in enumerate(near):
        @pl.when(met(me, n, k))
        def _():
            shift(i, k, 0).wait_send()
            shift(i, k, 1).wait_send()


def backward(n, cotangent, tokens, w_qkv, w_out, w_fc1, w_fc2, gain, bias, qkv_down, qkv_up, out_down, out_up, ff_down, fc1_up,
             fc2_down, fc2_up, adapters, saved):
    bf, f32 = jnp.bfloat16, jnp.float32
    r = ROWS_HERE
    outs = [((r, D), bf), ((3 * D, LANES), f32), ((3 * LANES, D), f32), ((D, LANES), f32), ((LANES, D), f32), ((D, LANES), f32),
            ((LANES, FP), f32), ((FP, LANES), f32), ((LANES, D), f32)]
    vmem = pl.BlockSpec(memory_space=pltpu.VMEM)
    away = pl.BlockSpec(memory_space=pl.ANY)
    dma = pltpu.SemaphoreType.DMA
    heads = (HEADS, HEAD_DIM, r)
    return pl.pallas_call(
        functools.partial(backward_kernel, n, adapters.shape[0]),
        out_shape=[jax.ShapeDtypeStruct(*o) for o in outs],
        in_specs=[vmem] * 2 + [away] * 4 + [vmem] * 10 + [pl.BlockSpec(memory_space=pltpu.SMEM)] + [vmem] * 3 + [away] + [vmem] * 9,
        out_specs=[vmem] * len(outs),
        scratch_shapes=[
            pltpu.VMEM((3 * D, D), bf), pltpu.VMEM((D, D), bf), pltpu.VMEM((2, D, STEP), bf), pltpu.VMEM((2, STEP, D), bf),
            pltpu.VMEM((2, 2, HEADS, r, HEAD_DIM), bf), pltpu.VMEM((2, HEADS, r, HEAD_DIM), bf),
            pltpu.VMEM((r, D), f32), pltpu.VMEM((r, D), f32), pltpu.VMEM((r, LANES), f32),
            pltpu.VMEM((SPAN,) + heads, bf), pltpu.VMEM((SPAN, HEADS, 8, r), f32),
            pltpu.VMEM(heads, f32), pltpu.VMEM(heads, f32), pltpu.VMEM(heads, f32),
            dma((2, 6)), dma((2, SPAN)), dma((3,)), dma((2,)), dma((2,)), dma((2,)),
        ],
        compiler_params=pltpu.CompilerParams(collective_id=2, has_side_effects=True, vmem_limit_bytes=63 << 20),
        name="layer_backward",
    )(cotangent, tokens, w_qkv, w_out, w_fc1, w_fc2, gain, bias, qkv_down, qkv_up, out_down, out_up, ff_down, fc1_up, fc2_down,
      fc2_up, adapters, *saved)


def local(
    tokens,
    qkv_weights,
    out_weights,
    fc1_weights,
    fc2_weights,
    ln_gain,
    bias_model,
    first_feedforward_bias,
    qkv_down,
    qkv_up,
    out_down,
    out_up,
    first_feedforward_down,
    fc1_up,
    fc2_down,
    fc2_up,
    adapter_of_image,
    cotangent,
):
    n = lax.axis_size("dp")
    w_qkv, w_out, w_fc1, w_fc2 = frozen(qkv_weights, out_weights, fc1_weights, fc2_weights)
    w_qkv = w_qkv.reshape(3 * D, D)
    tail = FP - FF
    fbias = jnp.pad(first_feedforward_bias, (0, tail))[None]
    fc1_up = jnp.pad(fc1_up, ((0, 0), (0, tail)))
    fc2_down = jnp.pad(fc2_down, ((0, tail), (0, 0)))
    factors = (qkv_down, qkv_up, out_down, out_up, first_feedforward_down, fc1_up, fc2_down, fc2_up, adapter_of_image)
    output, *saved = forward(n, tokens, w_qkv, w_out, w_fc1, w_fc2, ln_gain, bias_model, fbias, *factors)
    grad_tokens, *grads = backward(n, cotangent, tokens, w_qkv, w_out, w_fc1, w_fc2, ln_gain, bias_model, *factors, saved)
    grads[5] = grads[5][:, :FF]
    grads[6] = grads[6][:FF]
    summed = [lax.psum_scatter(g.reshape(-1), "dp", scatter_dimension=0, tiled=True) for g in grads]
    return (output, grad_tokens, *summed)


def solution(mesh):
    return jax.shard_map(
        local,
        mesh=mesh,
        in_specs=(P("dp", None),) + (P("dp"),) * 4 + (P(),) * 12 + (P("dp", None),),
        out_specs=(P("dp", None),) * 2 + (P("dp"),) * 8,
        check_vma=False,
    )
```

time: 911 us -> 703 us (0.77); the launches traced: 899 us -> 702 us
  Pallas kernels: 149 us -> 364 us
  matrix products: 162 us -> 0 us
  local copies, waits for them, and re-layouts: 179 us -> 37.7 us
  starting transfers between devices: 68.8 us -> 0.04 us
  other arithmetic: 46.8 us -> 1.28 us
    pallas_call x0 -> x2, Pallas kernels: none -> 215 us  [the longest x1 123 us: backward(): pl.pallas_call(functools.partial(backward_kernel, n, adapters.shape[0]),...]
    dot_general x59 -> x0, matrix products: 160 us -> none  [the longest x18 35.8 us: product_with_transpose(): lax.dot_general(left, right, (((1,), (1,)), ((), ())), preferred_element_...]
    unnamed x2, waiting for transfers between devices: 194 us -> 285 us
    ppermute x24 -> x0, waiting for transfers between devices: 82.9 us -> none  [shifted(): lax.ppermute(value, axis, [(source, source + steps) for source in range(f...]
    ppermute x24 -> x0, starting transfers between devices: 68.8 us -> none  [shifted(): lax.ppermute(value, axis, [(source, source + steps) for source in range(f...]
    dynamic_update_slice x4 -> x0, local copies, waits for them, and re-layouts: 58.1 us -> none  [the longest x2 29.1 us: local(): lax.dynamic_update_slice_in_dim(grad_ext_keys, lax.dynamic_slice_in_dim(g...]
    convert_element_type x14 -> x0, local copies, waits for them, and re-layouts: 26.1 us -> none  [the longest x3 6.5 us: local(): grad_ext_keys[high_begin:high_begin + rim_rows].astype(jnp.bfloat16)]
    slice x11 -> x0, local copies, waits for them, and re-layouts: 22.8 us -> none  [the longest x2 5.58 us: local(): grad_keys_f = grad_ext_keys[IMG - 1:IMG - 1 + local_rows]]
  transfers between devices with their start and end apart: 25 -> 1, of which waited for: 8 -> 1; matrix products, arithmetic and copies ran while one was open for 13% -> 0% of each run, Pallas kernels for 0% -> 0%
where the time goes in v2:
time: 703 us; the launch traced here: 702 us
  Pallas kernels  364 us (52%)
  waiting for transfers between devices  285 us (41%)
  local copies, waits for them, and re-layouts  37.7 us (5%)
  between operations  14.2 us (2%)
    unnamed x2, waiting for transfers between devices  285 us
    pallas_call x1, Pallas kernels, gather(): pl.pallas_call(functools.partial(gather_kernel, layers), out_shape=[jax.S...  149 us
    pallas_call x1, Pallas kernels, backward(): pl.pallas_call(functools.partial(backward_kernel, n, adapters.shape[0]),...  123 us
    pallas_call x1, Pallas kernels, forward(): pl.pallas_call(functools.partial(forward_kernel, n, adapters.shape[0]), o...  92.3 us
    unnamed x29, local copies, waits for them, and re-layouts  20 us
  transfers between devices with their start and end apart: 1, of which 1 were waited for; matrix products, arithmetic and copies ran while one was open for 0% of the time, Pallas kernels for 0%

profile of v2, /device:TPU:0, one launch (start us, length us, event | category | flops | bytes accessed | tf_op | source)
XLA Modules:
  0.0 701.7 jit_solution(6415643847672793014)
XLA Ops:
  7.2 0.0 copy-start.8
  7.2 0.0 all-reduce.17.cloned.1.call-start
  7.2 1.3 reshape.65.qkv
  8.5 1.0 reshape.66.out
  9.5 1.4 reshape.67
  10.9 1.3 pad_select_fusion
  12.2 0.4 reshape.68.fc2
  12.6 0.0 copy-done.8
  12.6 0.6 broadcast_in_dim.4.fbias
  13.2 0.0 copy-start.3
  13.2 1.8 copy.30
  15.0 1.1 pad.20.fc1_up
  16.1 0.0 copy-done.3
  16.1 1.1 pad.21.fc2_down
  17.2 149.1 %gather_weights.1 = (bf16[432,8,1152]{2,1,0:T(8,128)(2,1)S(1)}, bf16[144,8,1152]{2,1,0:T(8,128)(2,1)S(1)}, bf16[144,8,4352]{2,1,0:T(8,128)(2,1)}, bf16[544,8,1152]{2,1,0:T(8,128)(2,1)}) custom-call(bf16[108,1152]{1,0:T(8,128)(2,1)S(1)} %reshape.65.qkv, bf16[36,1152]{1,0:T(8,128)(2,1)S(1)} %reshape.66.out, bf16[36,4352]{1,0:T(8,128)(2,1)S(1)} %pad.18.fc1, ...), custom_call_target="tpu_custom_call" | custom-call | tf_op jit(solution)/shard_map/gather_weights/pallas_call | solution.py:244
  166.3 0.0 copy-start
  166.3 3.1 copy-done
  169.5 0.0 copy-start.1
  169.5 1.5 copy-done.1
  171.0 92.3 %layer_forward.1 = (bf16[256,1152]{1,0:T(8,128)(2,1)}, bf16[256,1152]{1,0:T(8,128)(2,1)}, bf16[3,256,128]{2,1,0:T(8,128)(2,1)}, bf16[7,16,72,256]{3,2,1,0:T(8,12...) custom-call(bf16[256,1152]{1,0:T(8,128)(2,1)} %tokens.3, ...), custom_call_target="tpu_custom_call" | custom-call | tf_op jit(solution)/shard_map/layer_forward/pallas_call | solution.py:518
  263.3 122.5 %layer_backward.1 = (bf16[256,1152]{1,0:T(8,128)(2,1)}, f32[3456,128]{1,0:T(8,128)}, f32[384,1152]{1,0:T(8,128)}, f32[1152,128]{1,0:T(8,128)}, f32[128,1152]{1,0...) custom-call(bf16[256,1152]{1,0:T(8,128)(2,1)} %cotangent.1, ...), custom_call_target="tpu_custom_call" | custom-call | tf_op jit(solution)/shard_map/layer_backward/pallas_call | solution.py:738
  385.9 0.0 copy-start.7
  385.9 0.0 copy-start.2
  385.9 2.7 reshape.73
  388.6 0.0 copy-done.7
  388.6 0.9 reshape.75
  389.4 0.0 copy-done.2
  389.4 3.2 reshape.77
  392.6 0.0 copy-start.6
  392.6 3.2 slice_bitcast_fusion
  395.8 0.0 copy-done.6
  395.8 0.9 reshape.79
  396.7 0.0 copy-start.4
  396.7 0.0 all-reduce.17.cloned.1.call-update
  396.7 0.0 copy-start.5
  396.7 284.5 %all-reduce.17.cloned.1.call-done = (f32[442368]{0:T(1024)}, f32[442368]{0:T(1024)}, f32[147456]{0:T(1024)}, f32[147456]{0:T(1024)}, f32[147456]{0:T(1024)}, /*i...) async-done(((f32[442368]{0:T(1024)}, f32[442368]{0:T(1024)}, f32[147456]{0:T(1024)}, f32[147456]{0:T(1024)}, f32[147456]{0:T(1024)}, /*index=5*/f32[550912]{0:T(1024)}, ...) | async-done | bytes 10305552
  681.2 1.5 dynamic-slice
  682.8 1.5 dynamic-slice.1
  684.3 1.4 dynamic-slice.2
  685.7 1.4 dynamic-slice.3
  687.1 1.4 dynamic-slice.4
  688.6 1.6 dynamic-slice.5
  690.2 1.6 dynamic-slice.6
  691.8 1.4 dynamic-slice.7
  693.2 0.0 copy-done.4
  693.2 0.8 copy.41
  694.0 0.0 copy-done.5
  694.0 0.8 copy.42
  (2 shorter events, 0.0 us)
Async XLA Ops:
  7.2 5.4 copy-start.8
  7.2 674.0 %all-reduce.17.cloned.1.call-start = ((), (), s32[]{:S(2)}) async-start(), calls=%async_computation | async-start | bytes 20611072
  13.2 2.9 copy-start.3
  166.3 3.1 copy-start
  169.5 1.5 copy-start.1
  385.9 2.7 copy-start.7
  385.9 3.6 copy-start.2
  392.6 3.2 copy-start.6
  396.7 296.5 %copy-start.4 = (bf16[256,1152]{1,0:T(8,128)(2,1)S(1)}, bf16[256,1152]{1,0:T(8,128)(2,1)}, u32[]{:S(2)}) copy-start(bf16[256,1152]{1,0:T(8,128)(2,1)} %get-tuple-element.82) | copy-start | bytes 1769476
  396.7 297.3 %copy-start.5 = (bf16[256,1152]{1,0:T(8,128)(2,1)S(1)}, bf16[256,1152]{1,0:T(8,128)(2,1)}, u32[]{:S(2)}) copy-start(bf16[256,1152]{1,0:T(8,128)(2,1)} %get-tuple-element.83) | copy-start | bytes 1769476
Sparse Core Ops, SparseCore 0:
  396.8 284.3 all-reduce.16

commit v3 on v2

--- a/solution.py
+++ b/solution.py
@@ -529,6 +529,9 @@
         name="layer_forward",
     )(tokens, w_qkv, w_out, w_fc1, w_fc2, gain, bias, fbias, qkv_down, qkv_up, out_down, out_up, ff_down, fc1_up, fc2_down,
       fc2_up, adapters)
+CHIPS = 16
+SLOTS = 2 * RANK
+DOWN = (3 * D, D, D, FP)
 
 
 def norm_back(center, inv, gain_row, grad):
@@ -540,16 +543,33 @@
 def backward_kernel(n, images, cotangent, tokens, w_qkv, w_out, w_fc1, w_fc2, gain, bias, qkv_down, qkv_up, out_down, out_up,
                     ff_down, fc1_up, fc2_down, fc2_up, adapters,
                     normed1, low_qkv, qt, kv, lse, mixed_t, mixed, low_out, resid, normed2, low_fc1, pre, low_fc2,
-                    grad_tokens, g_qkv_down, g_qkv_up, g_out_down, g_out_up, g_ff_down, g_fc1_up, g_fc2_down, g_fc2_up,
-                    v_qkv, v_out, v_fc1, v_fc2, v_kv, own_kv, wide, dres, acc, dat, stat, dq, dk, dv,
-                    send, recv, w_sem, fc1_sem, fc2_sem, kv_sem):
+                    grad_tokens, *rest):
+    reduce = n == 4 * PLANE
+    count = 8 if reduce else len(DOWN) + 1
+    results, rest = rest[:count], rest[count:]
+    (v_qkv, v_out, v_fc1, v_fc2, v_kv, own_kv, wide, dres, acc, dat, stat, dq, dk, dv,
+     send, recv, w_sem, fc1_sem, fc2_sem, kv_sem, v_pre, pre_sem), rest = rest[:22], rest[22:]
+    if reduce:
+        (ups, *downs), rest = rest[:5], rest[5:]
+        packed, mate_in, going, coming, final, mate_sem, far_send, far_recv, last_sem = (
+            rest[0:2], rest[2:6], rest[6:10], rest[10:14], rest[14:22], *rest[22:26])
+    else:
+        ups, *downs = results
+    g_qkv, g_out, g_ff, g_fc2 = downs
     me = lax.axis_index("dp")
+    core = lax.rem(me, 2)
+    chip = me // 2
+    mate = me + 1 - 2 * core
     own = pltpu.make_async_copy(kv.at[:, SIDE], own_kv, w_sem.at[0])
     own.start()
     get_out = pltpu.make_async_copy(w_out, v_out, w_sem.at[1])
     get_out.start()
-    get_qkv = pltpu.make_async_copy(w_qkv, v_qkv, w_sem.at[2])
-    get_qkv.start()
+
+    def fetch_qkv(t):
+        rows = pl.ds(t * COLS, COLS)
+        return pltpu.make_async_copy(w_qkv.at[rows, :], v_qkv.at[t % 2], w_sem.at[2 + t % 2])
+
+    fetch_qkv(0).start()
 
     def fetch1(i):
         slot = lax.rem(i, 2)
@@ -561,8 +581,14 @@
         rows = pl.ds(pl.multiple_of(i * STEP, STEP), STEP)
         return pltpu.make_async_copy(w_fc2.at[rows, :], v_fc2.at[slot], fc2_sem.at[slot])
 
+    def fetch_pre(i):
+        slot = lax.rem(i, 2)
+        cols = pl.ds(pl.multiple_of(i * STEP, STEP), STEP)
+        return pltpu.make_async_copy(pre.at[:, cols], v_pre.at[slot], pre_sem.at[slot])
+
     fetch1(0).start()
     fetch2(0).start()
+    fetch_pre(0).start()
     near = [k for k in range(-SIDE, SIDE + 1) if k]
     barrier = pltpu.get_barrier_semaphore()
     total = jnp.int32(0)
@@ -574,47 +600,72 @@
         def _():
             pl.semaphore_signal(barrier, inc=1, device_id=(me + k,), device_id_type=MESH)
 
+    if reduce:
+        for k in range(1, CHIPS):
+            pl.semaphore_signal(barrier, inc=1, device_id=(lax.rem(me + 2 * k, n),), device_id_type=MESH)
+        pl.semaphore_signal(barrier, inc=1, device_id=(mate,), device_id_type=MESH)
+        total = total + CHIPS
     begin, end = reach(me, n)
     bf = jnp.bfloat16
     select = chosen_columns(adapters, images, me, SIDE)
+
+    def narrow(glow):
+        if not reduce:
+            return glow
+        first = (chip * 2 * ROWS_HERE) // IMG
+        shape = (LANES, SLOTS)
+        lane = lax.broadcasted_iota(jnp.int32, shape, 1)
+        late = lane >= RANK
+        adapter = jnp.where(late, adapters[jnp.minimum(first + 1, images - 1)], adapters[first])
+        pick = lax.broadcasted_iota(jnp.int32, shape, 0) == adapter * RANK + lane - jnp.where(late, RANK, 0)
+        place = me * ROWS_HERE + lax.broadcasted_iota(jnp.int32, (ROWS_HERE, SLOTS), 0)
+        mine = (place >= (first + 1) * IMG) == (lax.broadcasted_iota(jnp.int32, (ROWS_HERE, SLOTS), 1) >= RANK)
+        return jnp.where(mine, mm(glow, pick.astype(bf)), 0.0).astype(bf)
+
+    def put_up(at, value):
+        ups[:, :, at] = value.reshape(CHIPS, 8, value.shape[-1])
+
     e = cotangent[...]
-    g_fc2_up[...] = t_mm(low_fc2[...], e)
+    put_up(slice(0, D), t_mm(low_fc2[...], e))
     glow2 = (select * mm_t(e, fc2_up[...])).astype(bf)
     acc[...] = jnp.zeros_like(acc)
     wide[...] = jnp.zeros_like(wide)
     low1 = low_fc1[...]
+    glow2n = narrow(glow2)
 
     def feed(i, carry):
         @pl.when(i + 1 < FP // STEP)
         def _():
             fetch1(i + 1).start()
             fetch2(i + 1).start()
+            fetch_pre(i + 1).start()
+        fetch_pre(i).wait()
         fetch1(i).wait()
         fetch2(i).wait()
         slot = lax.rem(i, 2)
         s = pl.ds(pl.multiple_of(i * STEP, STEP), STEP)
-        y = pre[:, s]
+        y = v_pre[slot]
         t = jnp.tanh(0.7978845608028654 * (y + 0.044715 * y * y * y))
         half = 0.5 * (1.0 + t)
         a = (y * half).astype(bf)
         slope = half + 0.5 * y * (1.0 - t * t) * (0.7978845608028654 * (1.0 + 3.0 * 0.044715 * y * y))
-        g_fc2_down[s, :] = t_mm(a, glow2)
+        g_fc2[:, s] = t_mm(glow2n, a)
         g = mm_t(e, v_fc2[slot]) + mm_t(glow2, fc2_down[s, :])
         gp = (g * slope).astype(bf)
-        g_fc1_up[:, s] = t_mm(low1, gp)
+        put_up(pl.ds(pl.multiple_of(D + i * STEP, LANES), STEP), t_mm(low1, gp))
         acc[...] += mm_t(gp, fc1_up[:, s])
         wide[...] += mm_t(gp, v_fc1[slot])
         return carry
 
     lax.fori_loop(0, FP // STEP, feed, 0)
     glow1 = (select * acc[...]).astype(bf)
-    g_ff_down[...] = t_mm(normed2[...], glow1)
+    g_ff[...] = t_mm(narrow(glow1), normed2[...])
     center, inv = moments(resid[...])
     dres[...] = e.astype(jnp.float32) + norm_back(center, inv, gain[1:2], wide[...] + mm_t(glow1, ff_down[...]))
     gb = dres[...].astype(bf)
-    g_out_up[...] = t_mm(low_out[...], gb)
+    put_up(slice(D + FP, 2 * D + FP), t_mm(low_out[...], gb))
     glow = (select * mm_t(gb, out_up[...])).astype(bf)
-    g_out_down[...] = t_mm(mixed[...], glow)
+    g_out[...] = t_mm(narrow(glow), mixed[...])
     get_out.wait()
     for c in range(0, D, COLS):
         wide[:, c:c + COLS] = mm_t(gb, v_out[c:c + COLS, :]) + mm_t(glow, out_down[c:c + COLS, :])
@@ -625,6 +676,106 @@
     stat[SIDE, :, 1:2, :] = delta
 
     pl.semaphore_wait(barrier, total)
+
+    half = CHIPS // 2
+    early = 2 * D + FP
+    if reduce:
+        upper = (ups.at[:, :, 0:early], ups.at[:, :, early:early + 3 * D])
+
+        def source(i):
+            return upper[i // 2] if i % 2 == 0 else packed[i // 2]
+
+        def to_mate(i):
+            return remote(source(i).at[pl.ds(half * (1 - core), half)], mate_in[i], mate_sem.at[0, i], mate_sem.at[1, i], mate)
+
+        def to_chip(i, k):
+            return remote(going[i].at[k], coming[i].at[chip], far_send.at[i, k], far_recv.at[i, chip], 2 * (half * core + k) + core)
+
+        def pass_on(i):
+            to_mate(i).wait_recv()
+
+            def one(k, carry):
+                going[i][k] = (source(i)[half * core + k] + mate_in[i][k]).astype(bf)
+
+                @pl.when(half * core + k != chip)
+                def _():
+                    to_chip(i, k).start()
+                return carry
+
+            lax.fori_loop(0, half, one, 0)
+
+            @pl.when(core == chip // half)
+            def _():
+                coming[i][chip] = going[i][chip - half * core]
+
+        def gathered(i):
+            for k in range(CHIPS):
+                @pl.when(chip != k)
+                def _():
+                    pltpu.make_async_copy(coming[i].at[k], coming[i].at[k], far_recv.at[i, k]).wait()
+
+        def add_up(i):
+            gathered(i)
+            return lax.fori_loop(1, CHIPS, lambda k, sofar: sofar + coming[i][k].astype(jnp.float32), coming[i][0].astype(jnp.float32))
+
+        def add_down(i):
+            gathered(i)
+            shape = (LANES, SLOTS)
+            lane = lax.broadcasted_iota(jnp.int32, shape, 1)
+            late = lane >= RANK
+            sofar = None
+            for k in range(CHIPS):
+                first = (k * 2 * ROWS_HERE) // IMG
+                adapter = jnp.where(late, adapters[min(first + 1, images - 1)], adapters[first])
+                pick = lax.broadcasted_iota(jnp.int32, shape, 0) == adapter * RANK + lane - jnp.where(late, RANK, 0)
+                part = mm(pick.astype(bf), coming[i][k])
+                sofar = part if k == 0 else sofar + part
+            return sofar.T
+
+        def flat_rows(ref, start, rows):
+            for t in range(D // LANES):
+                ref[pl.ds(start * (D // LANES) + t, rows.shape[0], stride=D // LANES), :] = rows[:, t * LANES:(t + 1) * LANES]
+
+        def hand_out(which):
+            for r in which:
+                results[r][...] = final[r][core]
+                remote(final[r].at[1 - core], results[r], last_sem.at[0, r], last_sem.at[1, r], mate).start()
+
+        (f_qkv_down, f_qkv_up, f_out_down, f_out_up, f_ff_down, f_fc1_up, f_fc2_down, f_fc2_up) = final
+
+        def finish_early():
+            v = add_up(0)
+            for q in range(2):
+                flat_rows(f_fc2_up.at[q], 0, v[4 * q:4 * q + 4, 0:D])
+                f_fc1_up[q] = v[4 * q:4 * q + 4, D:D + FP]
+                flat_rows(f_out_up.at[q], 0, v[4 * q:4 * q + 4, D + FP:2 * D + FP])
+            v = add_down(1)
+            f_fc2_down[0] = v[0:135]
+            turned = pltpu.roll(v, 64, axis=1)
+            left = lax.broadcasted_iota(jnp.int32, (135, LANES), 1) < 64
+            f_fc2_down[1] = jnp.where(left, turned[134:269], turned[135:270])
+            for q in range(2):
+                f_ff_down[q] = v[384 + 36 * q:420 + 36 * q]
+                f_out_down[q] = v[512 + 36 * q:548 + 36 * q]
+            hand_out((2, 3, 4, 5, 6, 7))
+
+        def finish_late():
+            v = add_up(2)
+            flat_rows(f_qkv_up.at[0], 0, v[:, 0:D])
+            flat_rows(f_qkv_up.at[0], 8, v[0:4, D:2 * D])
+            flat_rows(f_qkv_up.at[1], 0, v[4:8, D:2 * D])
+            flat_rows(f_qkv_up.at[1], 4, v[:, 2 * D:3 * D])
+            v = add_down(3)
+            for q in range(2):
+                f_qkv_down[q] = v[108 * q:108 * q + 108]
+            hand_out((0, 1))
+
+        for m in range(CHIPS):
+            packed[0][m, :, 0:269] = g_fc2[:, 269 * m:269 * m + 269]
+            packed[0][m, :, 384:456] = g_ff[:, 72 * m:72 * m + 72]
+            packed[0][m, :, 512:584] = g_out[:, 72 * m:72 * m + 72]
+        to_mate(0).start()
+        to_mate(1).start()
 
     def shift(i, k, what):
         ref = (dat, stat)[what]
@@ -665,6 +816,9 @@
 
     get_kv(begin).start()
     lax.fori_loop(0, HEADS, own_head, 0)
+    if reduce:
+        pass_on(0)
+        pass_on(1)
 
     def pass_one(j, carry):
         @pl.when(j < end)
@@ -704,18 +858,35 @@
         return carry
 
     lax.fori_loop(begin, end + 1, pass_two, 0)
-    get_qkv.wait()
     n1 = normed1[...]
-    for p, source in enumerate((dq, dk, dv)):
-        value = source[...] * HEAD_DIM ** (-0.5) if p < 2 else source[...]
+    grads = []
+    for p, total_grad in enumerate((dq, dk, dv)):
+        value = total_grad[...] * HEAD_DIM ** (-0.5) if p < 2 else total_grad[...]
         g = value.reshape(D, ROWS_HERE).T.astype(bf)
-        g_qkv_up[p * LANES:(p + 1) * LANES, :] = t_mm(low_qkv[p], g)
+        rows = t_mm(low_qkv[p], g)
+        for t in range(LANES // 8):
+            at = p * (LANES // 8) + t
+            ups[at // 3, :, early + at % 3 * D:early + at % 3 * D + D] = rows[8 * t:8 * t + 8]
         glow = (select * mm_t(g, qkv_up[p])).astype(bf)
-        g_qkv_down[p * D:(p + 1) * D, :] = t_mm(n1, glow)
+        g_qkv[:, p * D:(p + 1) * D] = t_mm(narrow(glow), n1)
+        grads.append((g, glow))
+    if reduce:
+        for m in range(CHIPS):
+            packed[1][m, :, 0:216] = g_qkv[:, 216 * m:216 * m + 216]
+        to_mate(2).start()
+        to_mate(3).start()
+    for p, (g, glow) in enumerate(grads):
         for c in range(0, D, COLS):
             s = slice(c, c + COLS)
-            y = mm_t(g, v_qkv[p * D + c:p * D + c + COLS, :]) + mm_t(glow, qkv_down[p, s, :])
+            t = (p * D + c) // COLS
+            if t + 1 < 3 * D // COLS:
+                fetch_qkv(t + 1).start()
+            fetch_qkv(t).wait()
+            y = mm_t(g, v_qkv[t % 2]) + mm_t(glow, qkv_down[p, s, :])
             wide[:, s] = y if p == 0 else wide[:, s] + y
+        if reduce and p == 0:
+            pass_on(2)
+            pass_on(3)
     center, inv = moments(tokens[...].astype(jnp.float32))
     grad_tokens[...] = (dres[...] + norm_back(center, inv, gain[0:1], wide[...])).astype(bf)
     for i, k in enumerate(near):
@@ -723,14 +894,50 @@
         def _():
             shift(i, k, 0).wait_send()
             shift(i, k, 1).wait_send()
+    if reduce:
+        reducer = core == chip // half
+
+        @pl.when(reducer)
+        def _():
+            finish_early()
+            finish_late()
+            for r in range(8):
+                remote(final[r].at[1 - core], results[r], last_sem.at[0, r], last_sem.at[1, r], mate).wait_send()
+
+        @pl.when(jnp.logical_not(reducer))
+        def _():
+            for r in range(8):
+                pltpu.make_async_copy(results[r], results[r], last_sem.at[1, r]).wait()
+
+        for i in range(4):
+            to_mate(i).wait_send()
+            for k in range(half):
+                @pl.when(half * core + k != chip)
+                def _():
+                    to_chip(i, k).wait_send()
 
 
 def backward(n, cotangent, tokens, w_qkv, w_out, w_fc1, w_fc2, gain, bias, qkv_down, qkv_up, out_down, out_up, ff_down, fc1_up,
              fc2_down, fc2_up, adapters, saved):
     bf, f32 = jnp.bfloat16, jnp.float32
     r = ROWS_HERE
-    outs = [((r, D), bf), ((3 * D, LANES), f32), ((3 * LANES, D), f32), ((D, LANES), f32), ((LANES, D), f32), ((D, LANES), f32),
-            ((LANES, FP), f32), ((FP, LANES), f32), ((LANES, D), f32)]
+    reduce = n == 4 * PLANE
+    deep = SLOTS if reduce else LANES
+    partial = [((CHIPS, 8, 5 * D + FP), f32)] + [((deep, w), f32) for w in DOWN]
+    shares = [(108, LANES), (108, LANES), (36, LANES), (36, LANES), (36, LANES), (4, FP), (135, LANES), (36, LANES)]
+    outs = [((r, D), bf)] + ([(s, f32) for s in shares] if reduce else partial)
+    more = []
+    if reduce:
+        half = CHIPS // 2
+        up, down = (2 * D + FP, 3 * D), (640, 256)
+        more = [pltpu.VMEM(*v) for v in partial]
+        more += [pltpu.VMEM((CHIPS, SLOTS, w), f32) for w in down]
+        for rows, kind in ((half, f32), (half, bf), (CHIPS, bf)):
+            for w, v in zip(up, down):
+                more += [pltpu.VMEM((rows, 8, w), kind), pltpu.VMEM((rows, SLOTS, v), kind)]
+        more += [pltpu.VMEM((2,) + s, f32) for s in shares]
+        dma = pltpu.SemaphoreType.DMA
+        more += [dma((2, 4)), dma((4, half)), dma((4, CHIPS)), dma((2, 8))]
     vmem = pl.BlockSpec(memory_space=pltpu.VMEM)
     away = pl.BlockSpec(memory_space=pl.ANY)
     dma = pltpu.SemaphoreType.DMA
@@ -738,16 +945,17 @@
     return pl.pallas_call(
         functools.partial(backward_kernel, n, adapters.shape[0]),
         out_shape=[jax.ShapeDtypeStruct(*o) for o in outs],
-        in_specs=[vmem] * 2 + [away] * 4 + [vmem] * 10 + [pl.BlockSpec(memory_space=pltpu.SMEM)] + [vmem] * 3 + [away] + [vmem] * 9,
+        in_specs=[vmem] * 2 + [away] * 4 + [vmem] * 10 + [pl.BlockSpec(memory_space=pltpu.SMEM)] + [vmem] * 3 + [away] + [vmem] * 7 + [away, vmem],
         out_specs=[vmem] * len(outs),
         scratch_shapes=[
-            pltpu.VMEM((3 * D, D), bf), pltpu.VMEM((D, D), bf), pltpu.VMEM((2, D, STEP), bf), pltpu.VMEM((2, STEP, D), bf),
+            pltpu.VMEM((2, COLS, D), bf), pltpu.VMEM((D, D), bf), pltpu.VMEM((2, D, STEP), bf), pltpu.VMEM((2, STEP, D), bf),
             pltpu.VMEM((2, 2, HEADS, r, HEAD_DIM), bf), pltpu.VMEM((2, HEADS, r, HEAD_DIM), bf),
             pltpu.VMEM((r, D), f32), pltpu.VMEM((r, D), f32), pltpu.VMEM((r, LANES), f32),
             pltpu.VMEM((SPAN,) + heads, bf), pltpu.VMEM((SPAN, HEADS, 8, r), f32),
             pltpu.VMEM(heads, f32), pltpu.VMEM(heads, f32), pltpu.VMEM(heads, f32),
-            dma((2, 6)), dma((2, SPAN)), dma((3,)), dma((2,)), dma((2,)), dma((2,)),
-        ],
+            dma((2, 6)), dma((2, SPAN)), dma((4,)), dma((2,)), dma((2,)), dma((2,)),
+            pltpu.VMEM((2, r, STEP), f32), dma((2,)),
+        ] + more,
         compiler_params=pltpu.CompilerParams(collective_id=2, has_side_effects=True, vmem_limit_bytes=63 << 20),
         name="layer_backward",
     )(cotangent, tokens, w_qkv, w_out, w_fc1, w_fc2, gain, bias, qkv_down, qkv_up, out_down, out_up, ff_down, fc1_up, fc2_down,
@@ -784,9 +992,25 @@
     factors = (qkv_down, qkv_up, out_down, out_up, first_feedforward_down, fc1_up, fc2_down, fc2_up, adapter_of_image)
     output, *saved = forward(n, tokens, w_qkv, w_out, w_fc1, w_fc2, ln_gain, bias_model, fbias, *factors)
     grad_tokens, *grads = backward(n, cotangent, tokens, w_qkv, w_out, w_fc1, w_fc2, ln_gain, bias_model, *factors, saved)
-    grads[5] = grads[5][:, :FF]
-    grads[6] = grads[6][:FF]
-    summed = [lax.psum_scatter(g.reshape(-1), "dp", scatter_dimension=0, tiled=True) for g in grads]
+    if n == 4 * PLANE:
+        grads[5] = grads[5][:, :FF]
+        summed = [g.reshape(-1) for g in grads]
+        summed[6] = summed[6][: FF * LANES // n]
+        return (output, grad_tokens, *summed)
+    ups, g_qkv, g_out, g_ff, g_fc2 = grads
+    early = 2 * D + FP
+    g_up = ups[:, :, early:].reshape(CHIPS, 8, 3, D).transpose(0, 2, 1, 3)
+    parts = (
+        g_qkv.T,
+        g_up,
+        g_out.T,
+        ups[:, :, D + FP : early],
+        g_ff.T,
+        ups[:, :, D : D + FF],
+        g_fc2.T[:FF],
+        ups[:, :, :D],
+    )
+    summed = [lax.psum_scatter(g.reshape(-1), "dp", scatter_dimension=0, tiled=True) for g in parts]
     return (output, grad_tokens, *summed)
 
 

time: 703 us -> 476 us (0.68)
  waiting for transfers between devices: 285 us -> 0 us
  Pallas kernels: 364 us -> 450 us
  local copies, waits for them, and re-layouts: 37.7 us -> 22.3 us
  between operations: 14.2 us -> 0.81 us
    unnamed x2 -> x0, waiting for transfers between devices: 285 us -> none
    pallas_call x1, Pallas kernels: 123 us -> 209 us  [backward(): pl.pallas_call(functools.partial(backward_kernel, n, adapters.shape[0]),...]
    reshape x5 -> x1, local copies, waits for them, and re-layouts: 10.8 us -> 1.69 us  [local(): summed = [g.reshape(-1) for g in grads]]
    unnamed x29 -> x34, local copies, waits for them, and re-layouts: 20 us -> 13.6 us
  transfers between devices with their start and end apart: 1 -> 0, of which waited for: 1 -> 0; matrix products, arithmetic and copies ran while one was open for 0% -> 0% of each run, Pallas kernels for 0% -> 0%
where the time goes in v3:
time: 476 us; the launch traced here: 475 us
  Pallas kernels  450 us (95%)
  local copies, waits for them, and re-layouts  22.3 us (5%)
    pallas_call x1, Pallas kernels, backward(): pl.pallas_call(functools.partial(backward_kernel, n, adapters.shape[0]),...  209 us
    pallas_call x1, Pallas kernels, gather(): pl.pallas_call(functools.partial(gather_kernel, layers), out_shape=[jax.S...  149 us
    pallas_call x1, Pallas kernels, forward(): pl.pallas_call(functools.partial(forward_kernel, n, adapters.shape[0]), o...  92.3 us
    unnamed x34, local copies, waits for them, and re-layouts  13.6 us

profile of v3, /device:TPU:0, one launch (start us, length us, event | category | flops | bytes accessed | tf_op | source)
XLA Modules:
  0.0 474.6 jit_solution(7670315753968149533)
XLA Ops:
  0.6 0.0 copy-start.11
  0.7 0.0 copy-start.3
  0.7 1.3 reshape.65.qkv
  2.0 1.0 reshape.66.out
  3.0 1.4 reshape.67
  4.5 1.3 pad_select_fusion
  5.8 0.4 reshape.68.fc2
  6.2 0.0 copy-start.2
  6.2 149.2 %gather_weights.1 = (bf16[432,8,1152]{2,1,0:T(8,128)(2,1)S(1)}, bf16[144,8,1152]{2,1,0:T(8,128)(2,1)S(1)}, bf16[144,8,4352]{2,1,0:T(8,128)(2,1)}, bf16[544,8,1152]{2,1,0:T(8,128)(2,1)}) custom-call(bf16[108,1152]{1,0:T(8,128)(2,1)S(1)} %reshape.65.qkv, bf16[36,1152]{1,0:T(8,128)(2,1)S(1)} %reshape.66.out, bf16[36,4352]{1,0:T(8,128)(2,1)S(1)} %pad.18.fc1, ...), custom_call_target="tpu_custom_call" | custom-call | tf_op jit(solution)/shard_map/gather_weights/pallas_call | solution.py:244
  155.3 0.0 copy-start
  155.3 3.2 copy-done
  158.5 0.0 copy-start.1
  158.5 1.5 copy-done.1
  160.0 0.0 copy-done.11
  160.0 0.6 broadcast_in_dim.4.fbias
  160.7 0.0 copy-done.3
  160.7 1.0 copy.28
  161.7 1.1 pad.20.fc1_up
  162.7 0.0 copy-done.2
  162.7 1.1 pad.21.fc2_down
  163.9 92.3 %layer_forward.1 = (bf16[256,1152]{1,0:T(8,128)(2,1)}, bf16[256,1152]{1,0:T(8,128)(2,1)}, bf16[3,256,128]{2,1,0:T(8,128)(2,1)}, bf16[7,16,72,256]{3,2,1,0:T(8,12...) custom-call(bf16[256,1152]{1,0:T(8,128)(2,1)} %tokens.3, ...), custom_call_target="tpu_custom_call" | custom-call | tf_op jit(solution)/shard_map/layer_forward/pallas_call | solution.py:518
  256.1 0.0 copy-start.4
  256.1 208.8 %layer_backward.1 = (bf16[256,1152]{1,0:T(8,128)(2,1)}, f32[108,128]{1,0:T(8,128)}, f32[108,128]{1,0:T(8,128)}, f32[36,128]{1,0:T(8,128)}, f32[36,128]{1,0:T(8,1...) custom-call(bf16[256,1152]{1,0:T(8,128)(2,1)} %cotangent.1, ...), custom_call_target="tpu_custom_call" | custom-call | tf_op jit(solution)/shard_map/layer_backward/pallas_call | solution.py:945
  464.9 0.0 copy-start.6
  465.0 0.0 copy-start.10
  465.0 0.0 copy-start.9
  465.0 0.0 copy-start.8
  465.0 0.0 copy-start.5
  465.0 0.0 copy-start.7
  465.0 1.7 reshape.77
  466.7 0.0 copy-done.4
  466.7 0.8 copy.38
  467.5 1.9 copy.39
  469.4 1.4 copy.40
  470.9 0.0 copy-done.6
  470.9 0.6 copy.41
  471.5 0.0 copy-done.10
  471.5 0.6 copy.42
  472.1 0.0 copy-done.9
  472.1 0.6 copy.43
  472.7 0.0 copy-done.8
  472.7 0.6 copy.44
  473.3 0.0 copy-done.5
  473.3 0.6 copy.45
  474.0 0.0 copy-done.7
  474.0 0.6 copy.46
  (2 shorter events, 0.0 us)
Async XLA Ops:
  0.6 159.4 %copy-start.11 = (f32[4304]{0:T(1024)S(1)}, f32[4304]{0:T(1024)}, u32[]{:S(2)}) copy-start(f32[4304]{0:T(1024)} %param.25) | copy-start | bytes 51652
  0.7 160.0 %copy-start.3 = (bf16[128,4304]{0,1:T(8,128)(2,1)S(1)}, bf16[128,4304]{0,1:T(8,128)(2,1)}, u32[]{:S(2)}) copy-start(bf16[128,4304]{0,1:T(8,128)(2,1)} %param.31) | copy-start | bytes 3305476
  6.2 156.6 %copy-start.2 = (bf16[4304,128]{1,0:T(8,128)(2,1)S(1)}, bf16[4304,128]{1,0:T(8,128)(2,1)}, u32[]{:S(2)}) copy-start(bf16[4304,128]{1,0:T(8,128)(2,1)} %param.32) | copy-start | bytes 3305476
  155.3 3.2 copy-start
  158.5 1.6 copy-start.1
  256.1 210.6 %copy-start.4 = (bf16[256,1152]{1,0:T(8,128)(2,1)S(1)}, bf16[256,1152]{1,0:T(8,128)(2,1)}, u32[]{:S(2)}) copy-start(bf16[256,1152]{1,0:T(8,128)(2,1)} %get-tuple-element.74) | copy-start | bytes 1769476
  464.9 5.9 %copy-start.6 = (f32[108,128]{1,0:T(8,128)S(1)}, f32[108,128]{1,0:T(8,128)}, u32[]{:S(2)}) copy-start(f32[108,128]{1,0:T(8,128)} %get-tuple-element.57) | copy-start | bytes 165892
  465.0 6.6 %copy-start.10 = (f32[36,128]{1,0:T(8,128)S(1)}, f32[36,128]{1,0:T(8,128)}, u32[]{:S(2)}) copy-start(f32[36,128]{1,0:T(8,128)} %get-tuple-element.58) | copy-start | bytes 55300
  465.0 7.2 %copy-start.9 = (f32[36,128]{1,0:T(8,128)S(1)}, f32[36,128]{1,0:T(8,128)}, u32[]{:S(2)}) copy-start(f32[36,128]{1,0:T(8,128)} %get-tuple-element.59) | copy-start | bytes 55300
  465.0 7.8 %copy-start.8 = (f32[36,128]{1,0:T(8,128)S(1)}, f32[36,128]{1,0:T(8,128)}, u32[]{:S(2)}) copy-start(f32[36,128]{1,0:T(8,128)} %get-tuple-element.60) | copy-start | bytes 55300
  465.0 8.4 %copy-start.5 = (f32[135,128]{1,0:T(8,128)S(1)}, f32[135,128]{1,0:T(8,128)}, u32[]{:S(2)}) copy-start(f32[135,128]{1,0:T(8,128)} %get-tuple-element.62) | copy-start | bytes 207364
  465.0 9.0 %copy-start.7 = (f32[36,128]{1,0:T(8,128)S(1)}, f32[36,128]{1,0:T(8,128)}, u32[]{:S(2)}) copy-start(f32[36,128]{1,0:T(8,128)} %get-tuple-element.63) | copy-start | bytes 55300
